TPU v7x, 512 devices: a whole 4x8x8 slice. The times are simulated.
512 devices in a mesh: freq: 32 (over z, y_hi, core), plane: 16 (over y_lo, x).
Axes of the slice: x: 4, y: 8 (y_hi: 2, y_lo: 4; y = y_hi * 4 + y_lo), z: 8, core: 2. Of those that a mesh axis runs over, the one named last changes fastest.
Arguments:
- contrast: float32 [2, 512, 2, 512], P(None, 'plane'), may hold values from -1 to 1
- green_kernel: bfloat16 [32, 2, 2, 2, 512, 512], P('freq', None, None, None, 'plane'), may hold values from -1 to 1
- source_pos: int32 [32, 2], P('freq'), may hold values from 0 to 511
- receiver_pos: int32 [32, 2, 64], P('freq'), may hold values from 0 to 511
- measured: float32 [32, 2, 64], P('freq'), may hold values from -6 to 6
Outputs:
- new_contrast: float32 [2, 512, 2, 512], P(None, 'plane')
- new_field: float32 [32, 2, 512, 2, 512], P('freq', None, 'plane')
Inputs may be any that keep to these rules, and one draw needn't show every extreme that they name: `source_pos`: row 0 is the x index and row 1 the y index of the source cell in layer 0. `receiver_pos`: row 0 holds the x indices and row 1 the y indices of the receiver cells in layer 0; receivers may coincide.
All inputs are finite; a program needn't handle non-finite values.
Results may differ from a plain program's by a relative error of at most 0.02.
Values may be sent and summed in bfloat16 or wider, within the bound.
No kernel may reach another device: no remote copies, remote signals or barrier semaphores. Data moves between devices by JAX's collectives and lax.ppermute only.
A program may use at most 64 MiB of HBM per device.

v0:
```python
import math

import jax
import jax.numpy as jnp
from jax import lax
from jax.sharding import PartitionSpec as P

ITERS = 2


source_gain = 3.0


def from_everyone(shard, axis):
    copies = jnp.broadcast_to(shard, (lax.axis_size(axis), *shard.shape))
    return lax.all_to_all(copies, axis, split_axis=0, concat_axis=0, tiled=True)


def taken_together(shard, axis):
    everything = from_everyone(shard, axis)
    return jnp.sum(everything, axis=0)


def split_up(shard, dim, peers):
    before, after = (shard.shape[:dim], shard.shape[dim + 1 :])
    return jnp.moveaxis(shard.reshape(*before, peers, -1, *after), dim, 0)


def summed_on_arrival(shard, axis, dim):
    parts = split_up(shard, dim, lax.axis_size(axis))
    arrived = lax.all_to_all(parts, axis, split_axis=0, concat_axis=0, tiled=True)
    return arrived.astype(jnp.float32).sum(axis=0)


def joined_along(parts, dim):
    parts = jnp.moveaxis(parts, 0, dim)
    lengths = parts.shape
    return parts.reshape(*lengths[:dim], lengths[dim] * lengths[dim + 1], *lengths[dim + 2 :])


def gathered_copies(shard, axis, dim):
    parts = from_everyone(shard, axis)
    return joined_along(parts, dim)


def phase_tables(length, out_type):
    positions = lax.iota(jnp.int32, length)
    turn_count = positions[:, None] * positions[None, :] % length
    angles = turn_count.astype(jnp.float32) * (2.0 * math.pi / length)
    norm_scale = 1.0 / math.sqrt(length)
    return jnp.concatenate(
        [jnp.cos(angles) * norm_scale, jnp.sin(angles) * norm_scale], axis=1
    ).astype(out_type)


def line_phase(positions, location, length):
    turn_count = positions * location % length
    angles = turn_count.astype(jnp.float32) * (2.0 * math.pi / length)
    return (jnp.cos(angles), -jnp.sin(angles))


def complex_product(first, second):
    return jnp.stack(
        [first[0] * second[0] - first[1] * second[1], first[0] * second[1] + first[1] * second[0]]
    )


def forward(wave_field, dft_table):
    row_count, layer_count, grid_size = wave_field.shape[1:]
    narrowed = wave_field.astype(jnp.bfloat16)
    products = jnp.dot(
        narrowed.reshape(2 * row_count * layer_count, grid_size),
        dft_table,
        preferred_element_type=jnp.float32,
    )
    products = products.reshape(2, row_count, layer_count, 2, grid_size)
    real_part = products[0, :, :, 0] + products[1, :, :, 1]
    imag_part = products[1, :, :, 0] - products[0, :, :, 1]
    narrowed = jnp.stack([real_part, imag_part]).astype(jnp.bfloat16)
    arrived = lax.all_to_all(narrowed, "plane", split_axis=3, concat_axis=1, tiled=True)
    col_count = arrived.shape[3]
    merged = arrived.reshape(2, grid_size, layer_count * col_count)
    products = jnp.einsum("cxq,xk->cqk", merged, dft_table, preferred_element_type=jnp.float32)
    real_part = products[0, :, :grid_size] + products[1, :, grid_size:]
    imag_part = products[1, :, :grid_size] - products[0, :, grid_size:]
    return jnp.stack([real_part, imag_part]).reshape(2, layer_count, col_count, grid_size)


def inverse(spectrum, dft_table):
    layer_count, col_count, grid_size = spectrum.shape[1:]
    narrowed = spectrum.astype(jnp.bfloat16).reshape(2, layer_count * col_count, grid_size)
    products = jnp.einsum("cqk,kt->ctq", narrowed, dft_table, preferred_element_type=jnp.float32)
    real_part = products[0, :grid_size] - products[1, grid_size:]
    imag_part = products[1, :grid_size] + products[0, grid_size:]
    narrowed = (
        jnp.stack([real_part, imag_part])
        .astype(jnp.bfloat16)
        .reshape(2, grid_size, layer_count, col_count)
    )
    arrived = lax.all_to_all(narrowed, "plane", split_axis=1, concat_axis=3, tiled=True)
    row_count = arrived.shape[1]
    products = jnp.dot(
        arrived.reshape(2 * row_count * layer_count, grid_size),
        dft_table,
        preferred_element_type=jnp.float32,
    )
    products = products.reshape(2, row_count, layer_count, 2, grid_size)
    real_part = products[0, :, :, 0] - products[1, :, :, 1]
    imag_part = products[1, :, :, 0] + products[0, :, :, 1]
    return jnp.stack([real_part, imag_part])


def couple(spectrum, kernel):
    layer_count = spectrum.shape[1]
    real_rows = []
    imag_rows = []
    for out_layer in range(layer_count):
        sum_real = jnp.zeros(spectrum.shape[2:], jnp.float32)
        sum_imag = jnp.zeros(spectrum.shape[2:], jnp.float32)
        for in_layer in range(layer_count):
            kern_real = kernel[0, out_layer, in_layer].astype(jnp.float32)
            kern_imag = kernel[1, out_layer, in_layer].astype(jnp.float32)
            sum_real = (
                sum_real + kern_real * spectrum[0, in_layer] - kern_imag * spectrum[1, in_layer]
            )
            sum_imag = (
                sum_imag + kern_real * spectrum[1, in_layer] + kern_imag * spectrum[0, in_layer]
            )
        real_rows.append(sum_real)
        imag_rows.append(sum_imag)
    return jnp.stack([jnp.stack(real_rows), jnp.stack(imag_rows)])


def green_apply(wave_field, kernel, dft_table):
    return inverse(couple(forward(wave_field, dft_table), kernel), dft_table)


def local(contrast, green_kernel, source_pos, receiver_pos, measured):
    freq_count = green_kernel.shape[0]
    row_count = contrast.shape[1]
    grid_size = contrast.shape[3]
    dft_table = phase_tables(grid_size, jnp.bfloat16)
    first_row = lax.axis_index("plane") * row_count
    own_rows = first_row + lax.iota(jnp.int32, row_count)
    all_cols = lax.iota(jnp.int32, grid_size)
    which = 0
    kernel = green_kernel[which]
    phase_y_real, phase_y_imag = line_phase(own_rows, source_pos[which, 1], grid_size)
    phase_x_real, phase_x_imag = line_phase(all_cols, source_pos[which, 0], grid_size)
    source_real = source_gain * (
        phase_y_real[:, None] * phase_x_real[None, :]
        - phase_y_imag[:, None] * phase_x_imag[None, :]
    )
    source_imag = source_gain * (
        phase_y_real[:, None] * phase_x_imag[None, :]
        + phase_y_imag[:, None] * phase_x_real[None, :]
    )
    column_zero = kernel[:, :, 0].astype(jnp.float32)
    spectrum = jnp.stack(
        [
            column_zero[0] * source_real - column_zero[1] * source_imag,
            column_zero[0] * source_imag + column_zero[1] * source_real,
        ]
    )
    incident = inverse(spectrum, dft_table)
    wave_field = incident
    for sweep_index in range(ITERS):
        wave_field = incident + green_apply(
            complex_product(contrast, wave_field), kernel, dft_table
        )
    recv_x = receiver_pos[which, 0]
    recv_y = receiver_pos[which, 1]
    pick_rows = (recv_x[:, None] == own_rows[None, :]).astype(jnp.float32)
    pick_cols = (recv_y[:, None] == all_cols[None, :]).astype(jnp.float32)
    surface = jnp.einsum("rx,cxy->cry", pick_rows, wave_field[:, :, 0, :])
    sampled = jnp.sum(surface * pick_cols[None], axis=2)
    gathered = taken_together(sampled, "plane")
    misfit = gathered - measured[which]
    recv_y_real, recv_y_imag = line_phase(own_rows[None, :], recv_y[:, None], grid_size)
    recv_x_real, recv_x_imag = line_phase(all_cols[None, :], recv_x[:, None], grid_size)
    mixed_real = misfit[0][:, None] * recv_y_real - misfit[1][:, None] * recv_y_imag
    mixed_imag = misfit[0][:, None] * recv_y_imag + misfit[1][:, None] * recv_y_real
    contract = (((0,), (0,)), ((), ()))
    adj_real = lax.dot_general(
        mixed_real, recv_x_real, contract, preferred_element_type=jnp.float32
    ) - lax.dot_general(mixed_imag, recv_x_imag, contract, preferred_element_type=jnp.float32)
    adj_imag = lax.dot_general(
        mixed_real, recv_x_imag, contract, preferred_element_type=jnp.float32
    ) + lax.dot_general(mixed_imag, recv_x_real, contract, preferred_element_type=jnp.float32)
    row_zero = kernel[:, 0].astype(jnp.float32)
    back_spec = jnp.stack(
        [
            row_zero[0] * adj_real + row_zero[1] * adj_imag,
            row_zero[0] * adj_imag - row_zero[1] * adj_real,
        ]
    )
    backward = inverse(back_spec, dft_table)
    gradient = jnp.stack(
        [
            wave_field[0] * backward[0] + wave_field[1] * backward[1],
            wave_field[0] * backward[1] - wave_field[1] * backward[0],
        ]
    )
    incidents = [incident]
    solutions = [wave_field]
    total_freqs = freq_count * lax.axis_size("freq")
    own_share = summed_on_arrival(gradient.astype(jnp.bfloat16), "freq", 3)
    share_cols = own_share.shape[3]
    own_contrast = lax.dynamic_slice_in_dim(
        contrast, lax.axis_index("freq") * share_cols, share_cols, 3
    )
    updated = gathered_copies(own_contrast - own_share / total_freqs, "freq", 3)
    which = 0
    outputs = [
        incidents[which]
        + green_apply(complex_product(updated, solutions[which]), green_kernel[which], dft_table)
    ]
    return (updated, jnp.stack(outputs))


def solution(mesh):
    return jax.shard_map(
        local,
        mesh=mesh,
        in_specs=(
            P(None, "plane", None, None),
            P("freq", None, None, None, "plane", None),
            P("freq", None),
            P("freq", None, None),
            P("freq", None, None),
        ),
        out_specs=(P(None, "plane", None, None), P("freq", None, "plane", None, None)),
        check_vma=False,
    )
```

profile of v0, /device:TPU:2, one launch (start us, length us, event | category | flops | bytes accessed | tf_op | source)
XLA Modules:
  0.0 229.3 jit_solution(7252167261015452433)
XLA Ops:
  0.7 4.4 %multiply_convert_fusion = (bf16[512,512]{1,0:T(8,128)(2,1)S(1)}, bf16[512,512]{1,0:T(8,128)(2,1)S(1)}) fusion(), kind=kLoop, calls=%fused_computation.29 | loop fusion | flops 4718592 | bytes 1048576 | tf_op jit(solution)/shard_map/convert.83
  9.4 9.8 %all-to-all-start = ((bf16[16,2,2048]{2,1,0:T(2,128)(2,1)}), bf16[16,2,2048]{2,1,0:T(2,128)(2,1)}, u32[]{:S(2)}, u32[]{:S(2)}) async-start(bf16[16,2,2048]{2,1,0:T(2,128)(2,1)} %reshape.1604), calls=%async_computation | async-start | bytes 262144 | tf_op jit(solution)/shard_map/all_to_all | solution.py:100
  22.3 4.6 %all-to-all-done = bf16[16,2,2048]{2,1,0:T(2,128)(2,1)} async-done(((bf16[16,2,2048]{2,1,0:T(2,128)(2,1)}), bf16[16,2,2048]{2,1,0:T(2,128)(2,1)}, u32[]{:S(2)}, u32[]{:S(2)}) %all-to-all-start) | async-done | bytes 131104 | tf_op jit(solution)/shard_map/all_to_all | solution.py:100
  33.4 11.5 %all_to_all.135 = bf16[16,2,2048]{2,1,0:T(2,128)(2,1)S(1)} all-to-all(bf16[16,2,2048]{2,1,0:T(2,128)(2,1)S(1)} %reshape.1606), channel_id=1, replica_groups=mesh['freq'=32,'plane'=16] {'plane'}, dimensions={0} | all-to-all | bytes 262144 | tf_op jit(solution)/shard_map/all_to_all | solution.py:80
  46.0 1.5 fusion.13
  50.7 5.3 %all-to-all-start.2 = ((bf16[16,2,2048]{2,1,0:T(2,128)(2,1)}), bf16[16,2,2048]{2,1,0:T(2,128)(2,1)}, u32[]{:S(2)}, u32[]{:S(2)}) async-start(bf16[16,2,2048]{2,1,0:T(2,128)(2,1)} %reshape.1608), calls=%async_computation.2 | async-start | bytes 262144 | tf_op jit(solution)/shard_map/all_to_all | solution.py:100
  57.5 6.3 %all-to-all-done.2 = bf16[16,2,2048]{2,1,0:T(2,128)(2,1)} async-done(((bf16[16,2,2048]{2,1,0:T(2,128)(2,1)}), bf16[16,2,2048]{2,1,0:T(2,128)(2,1)}, u32[]{:S(2)}, u32[]{:S(2)}) %all-to-all-start.2) | async-done | bytes 131104 | tf_op jit(solution)/shard_map/all_to_all | solution.py:100
  69.5 4.8 %all-to-all-start.3 = ((bf16[16,2,2048]{2,1,0:T(2,128)(2,1)}), bf16[16,2,2048]{2,1,0:T(2,128)(2,1)S(1)}, u32[]{:S(2)}, u32[]{:S(2)}) async-start(bf16[16,2,2048]{2,1,0:T(2,128)(2,1)} %reshape.1610), calls=%async_computation.3 | async-start | bytes 262144 | tf_op jit(solution)/shard_map/all_to_all | solution.py:80
  74.3 7.6 %all-to-all-done.3 = bf16[16,2,2048]{2,1,0:T(2,128)(2,1)S(1)} async-done(((bf16[16,2,2048]{2,1,0:T(2,128)(2,1)}), bf16[16,2,2048]{2,1,0:T(2,128)(2,1)S(1)}, u32[]{:S(2)}, u32[]{:S(2)}) %all-to-all-start.3) | async-done | bytes 131104 | tf_op jit(solution)/shard_map/all_to_all | solution.py:80
  83.0 1.5 fusion.10
  87.7 4.8 %all-to-all-start.4 = ((bf16[16,2,2048]{2,1,0:T(2,128)(2,1)}), bf16[16,2,2048]{2,1,0:T(2,128)(2,1)S(1)}, u32[]{:S(2)}, u32[]{:S(2)}) async-start(bf16[16,2,2048]{2,1,0:T(2,128)(2,1)} %reshape.1612), calls=%async_computation.4 | async-start | bytes 262144 | tf_op jit(solution)/shard_map/all_to_all | solution.py:100
  92.5 7.6 %all-to-all-done.4 = bf16[16,2,2048]{2,1,0:T(2,128)(2,1)S(1)} async-done(((bf16[16,2,2048]{2,1,0:T(2,128)(2,1)}), bf16[16,2,2048]{2,1,0:T(2,128)(2,1)S(1)}, u32[]{:S(2)}, u32[]{:S(2)}) %all-to-all-start.4) | async-done | bytes 131104 | tf_op jit(solution)/shard_map/all_to_all | solution.py:100
  103.3 4.7 %all-to-all-start.5 = ((f32[16,1,128]{2,1,0:T(1,128)}), f32[16,1,128]{2,1,0:T(1,128)S(1)}, u32[]{:S(2)}, u32[]{:S(2)}) async-start(f32[16,1,128]{2,1,0:T(1,128)} %reshape.1614), calls=%async_computation.5 | async-start | bytes 16384 | tf_op jit(solution)/shard_map/all_to_all | solution.py:16
  108.0 6.5 %all-to-all-done.5 = f32[16,1,128]{2,1,0:T(1,128)S(1)} async-done(((f32[16,1,128]{2,1,0:T(1,128)}), f32[16,1,128]{2,1,0:T(1,128)S(1)}, u32[]{:S(2)}, u32[]{:S(2)}) %all-to-all-start.5) | async-done | bytes 8224 | tf_op jit(solution)/shard_map/all_to_all | solution.py:16
  120.4 11.5 %all_to_all.136 = bf16[16,2,2048]{2,1,0:T(2,128)(2,1)S(1)} all-to-all(bf16[16,2,2048]{2,1,0:T(2,128)(2,1)S(1)} %reshape.1616), channel_id=1, replica_groups=mesh['freq'=32,'plane'=16] {'plane'}, dimensions={0} | all-to-all | bytes 262144 | tf_op jit(solution)/shard_map/all_to_all | solution.py:100
  137.1 11.3 %all-to-all-start.7 = ((bf16[32,2,1024]{2,1,0:T(2,128)(2,1)}), bf16[32,2,1024]{2,1,0:T(2,128)(2,1)S(1)}, u32[]{:S(2)}, u32[]{:S(2)}) async-start(bf16[32,2,1024]{2,1,0:T(2,128)(2,1)} %reshape.1618), calls=%async_computation.7 | async-start | bytes 262144 | tf_op jit(solution)/shard_map/all_to_all | solution.py:31
  149.4 11.5 %all-to-all-done.7 = bf16[32,2,1024]{2,1,0:T(2,128)(2,1)S(1)} async-done(((bf16[32,2,1024]{2,1,0:T(2,128)(2,1)}), bf16[32,2,1024]{2,1,0:T(2,128)(2,1)S(1)}, u32[]{:S(2)}, u32[]{:S(2)}) %all-to-all-start.7) | async-done | bytes 131104 | tf_op jit(solution)/shard_map/all_to_all | solution.py:31
  162.6 18.3 %all_to_all.137 = f32[32,1,2048]{2,1,0:T(1,128)S(1)} all-to-all(f32[32,1,2048]{2,1,0:T(1,128)} %reshape.1620), channel_id=1, replica_groups=mesh['freq'=32,'plane'=16] {'freq'}, dimensions={0} | all-to-all | bytes 524288 | tf_op jit(solution)/shard_map/all_to_all | solution.py:16
  187.8 1.9 copy.353
  189.7 1.9 copy.354
  194.1 14.5 %all_to_all.138 = bf16[16,2,2048]{2,1,0:T(2,128)(2,1)S(1)} all-to-all(bf16[16,2,2048]{2,1,0:T(2,128)(2,1)S(1)} %reshape.1622), channel_id=1, replica_groups=mesh['freq'=32,'plane'=16] {'plane'}, dimensions={0} | all-to-all | bytes 262144 | tf_op jit(solution)/shard_map/all_to_all | solution.py:80
  209.7 1.5 fusion.6
  214.4 4.8 %all-to-all-start.10 = ((bf16[16,2,2048]{2,1,0:T(2,128)(2,1)}), bf16[16,2,2048]{2,1,0:T(2,128)(2,1)S(1)}, u32[]{:S(2)}, u32[]{:S(2)}) async-start(bf16[16,2,2048]{2,1,0:T(2,128)(2,1)} %reshape.1624), calls=%async_computation.10 | async-start | bytes 262144 | tf_op jit(solution)/shard_map/all_to_all | solution.py:100
  220.3 6.5 %all-to-all-done.10 = bf16[16,2,2048]{2,1,0:T(2,128)(2,1)S(1)} async-done(((bf16[16,2,2048]{2,1,0:T(2,128)(2,1)}), bf16[16,2,2048]{2,1,0:T(2,128)(2,1)S(1)}, u32[]{:S(2)}, u32[]{:S(2)}) %all-to-all-start.10) | async-done | bytes 131104 | tf_op jit(solution)/shard_map/all_to_all | solution.py:100
  (201 shorter events, 62.9 us)
Async XLA Ops:
  0.6 4.4 %copy-start.23 = (s32[1,2]{1,0:T(1,128)S(1)}, s32[1,2]{1,0:T(1,128)}, u32[]{:S(2)}) copy-start(s32[1,2]{1,0:T(1,128)} %param.7) | copy-start | bytes 28
  0.6 5.8 %copy-start.2 = (bf16[1,2,2,2,32,512]{5,4,3,2,1,0:T(8,128)(2,1)S(1)}, bf16[1,2,2,2,32,512]{5,4,3,2,1,0:T(8,128)(2,1)}, u32[]{:S(2)}) copy-start(bf16[1,2,2,2,32,512]{5,4,3,2,1,0:T(8,128)(2,1)} %param.6) | copy-start | bytes 786436
  5.1 14.1 %copy-start.6 = (bf16[512,512]{1,0:T(8,128)(2,1)}, bf16[512,512]{1,0:T(8,128)(2,1)S(1)}, u32[]{:S(2)}) copy-start(bf16[512,512]{1,0:T(8,128)(2,1)S(1)} %get-tuple-element.75) | copy-start | bytes 1572868
  5.1 14.1 %copy-start.11 = (bf16[512,512]{1,0:T(8,128)(2,1)}, bf16[512,512]{1,0:T(8,128)(2,1)S(1)}, u32[]{:S(2)}) copy-start(bf16[512,512]{1,0:T(8,128)(2,1)S(1)} %get-tuple-element.76) | copy-start | bytes 1572868
  9.4 17.6 %all-to-all-start = ((bf16[16,2,2048]{2,1,0:T(2,128)(2,1)}), bf16[16,2,2048]{2,1,0:T(2,128)(2,1)}, u32[]{:S(2)}, u32[]{:S(2)}) async-start(bf16[16,2,2048]{2,1,0:T(2,128)(2,1)} %reshape.1604), calls=%async_computation | async-start | bytes 262144 | tf_op jit(solution)/shard_map/all_to_all | solution.py:100
  20.1 1.5 copy-start.22
  29.6 1.4 copy-start.4
  31.0 1.4 copy-start
  47.5 1.0 copy-start.7
  47.5 1.2 copy-start.12
  50.7 13.1 %all-to-all-start.2 = ((bf16[16,2,2048]{2,1,0:T(2,128)(2,1)}), bf16[16,2,2048]{2,1,0:T(2,128)(2,1)}, u32[]{:S(2)}, u32[]{:S(2)}) async-start(bf16[16,2,2048]{2,1,0:T(2,128)(2,1)} %reshape.1608), calls=%async_computation.2 | async-start | bytes 262144 | tf_op jit(solution)/shard_map/all_to_all | solution.py:100
  67.9 6.4 %copy-start.25 = (s32[1,2,64]{2,1,0:T(2,128)S(1)}, s32[1,2,64]{2,1,0:T(2,128)}, u32[]{:S(2)}) copy-start(s32[1,2,64]{2,1,0:T(2,128)} %param.8) | copy-start | bytes 1540
  69.5 12.4 %all-to-all-start.3 = ((bf16[16,2,2048]{2,1,0:T(2,128)(2,1)}), bf16[16,2,2048]{2,1,0:T(2,128)(2,1)S(1)}, u32[]{:S(2)}, u32[]{:S(2)}) async-start(bf16[16,2,2048]{2,1,0:T(2,128)(2,1)} %reshape.1610), calls=%async_computation.3 | async-start | bytes 262144 | tf_op jit(solution)/shard_map/all_to_all | solution.py:80
  84.5 1.2 copy-start.13
  87.7 12.4 %all-to-all-start.4 = ((bf16[16,2,2048]{2,1,0:T(2,128)(2,1)}), bf16[16,2,2048]{2,1,0:T(2,128)(2,1)S(1)}, u32[]{:S(2)}, u32[]{:S(2)}) async-start(bf16[16,2,2048]{2,1,0:T(2,128)(2,1)} %reshape.1612), calls=%async_computation.4 | async-start | bytes 262144 | tf_op jit(solution)/shard_map/all_to_all | solution.py:100
  101.7 14.2 %copy-start.24 = (f32[1,2,64]{2,1,0:T(2,128)S(1)}, f32[1,2,64]{2,1,0:T(2,128)}, u32[]{:S(2)}) copy-start(f32[1,2,64]{2,1,0:T(2,128)} %param.9) | copy-start | bytes 1540
  102.2 33.1 %copy-start.3 = (f32[2,32,2,512]{3,1,2,0:T(8,128)}, f32[2,32,2,512]{3,1,2,0:T(8,128)S(1)}, u32[]{:S(2)}) copy-start(f32[2,32,2,512]{3,1,2,0:T(8,128)S(1)} %maximum_add_fusion.1) | copy-start | bytes 786436
  103.3 11.3 %all-to-all-start.5 = ((f32[16,1,128]{2,1,0:T(1,128)}), f32[16,1,128]{2,1,0:T(1,128)S(1)}, u32[]{:S(2)}, u32[]{:S(2)}) async-start(f32[16,1,128]{2,1,0:T(1,128)} %reshape.1614), calls=%async_computation.5 | async-start | bytes 16384 | tf_op jit(solution)/shard_map/all_to_all | solution.py:16
  117.4 1.6 copy-start.9
  117.4 1.6 copy-start.14
  137.1 23.9 %all-to-all-start.7 = ((bf16[32,2,1024]{2,1,0:T(2,128)(2,1)}), bf16[32,2,1024]{2,1,0:T(2,128)(2,1)S(1)}, u32[]{:S(2)}, u32[]{:S(2)}) async-start(bf16[32,2,1024]{2,1,0:T(2,128)(2,1)} %reshape.1618), calls=%async_computation.7 | async-start | bytes 262144 | tf_op jit(solution)/shard_map/all_to_all | solution.py:31
  211.2 1.2 copy-start.15
  212.7 6.4 %copy-start.1 = (f32[2,32,2,2,512]{4,1,3,2,0:T(8,128)S(1)}, f32[2,32,2,2,512]{4,1,3,2,0:T(8,128)}, u32[]{:S(2)}) copy-start(f32[2,32,2,2,512]{4,1,3,2,0:T(8,128)} %copy-done) | copy-start | bytes 1572868
  214.4 12.4 %all-to-all-start.10 = ((bf16[16,2,2048]{2,1,0:T(2,128)(2,1)}), bf16[16,2,2048]{2,1,0:T(2,128)(2,1)S(1)}, u32[]{:S(2)}, u32[]{:S(2)}) async-start(bf16[16,2,2048]{2,1,0:T(2,128)(2,1)} %reshape.1624), calls=%async_computation.10 | async-start | bytes 262144 | tf_op jit(solution)/shard_map/all_to_all | solution.py:100
  (9 other events, 8.2 us)
where the time goes:
time: 231 us; the launch traced here: 229 us
  blocking collectives  55.8 us (24%)
  waiting for transfers between devices  50.7 us (22%)
  local copies, waits for them, and re-layouts  50.4 us (22%)
  starting transfers between devices  45.4 us (20%)
  matrix products  14.2 us (6%)
  other arithmetic  11 us (5%)
    all_to_all x2, blocking collectives, forward(): lax.all_to_all(narrowed, 'plane', split_axis=3, concat_axis=1, tiled=True)  26 us
    all_to_all x4, waiting for transfers between devices, inverse(): lax.all_to_all(narrowed, 'plane', split_axis=1, concat_axis=3, tiled=True)  25 us
    all_to_all x4, starting transfers between devices, inverse(): lax.all_to_all(narrowed, 'plane', split_axis=1, concat_axis=3, tiled=True)  24.7 us
    unnamed x78, local copies, waits for them, and re-layouts  23.3 us
    all_to_all x1, blocking collectives, from_everyone(): return lax.all_to_all(copies, axis, split_axis=0, concat_axis=0, tiled=True)  18.3 us
    all_to_all x1, waiting for transfers between devices, summed_on_arrival(): lax.all_to_all(parts, axis, split_axis=0, concat_axis=0, tiled=True)  11.5 us
    all_to_all x1, blocking collectives, inverse(): lax.all_to_all(narrowed, 'plane', split_axis=1, concat_axis=3, tiled=True)  11.5 us
    all_to_all x1, starting transfers between devices, summed_on_arrival(): lax.all_to_all(parts, axis, split_axis=0, concat_axis=0, tiled=True)  11.3 us
  transfers between devices with their start and end apart: 7, of which 7 were waited for; matrix products, arithmetic and copies ran while one was open for 3% of the time, Pallas kernels for 0%

commit v1 on v0

v1 whole, which is shorter than its diff:
```python
import math

import jax
import jax.numpy as jnp
import ml_dtypes
import numpy as np
from jax import lax
from jax.experimental import pallas as pl
from jax.experimental.pallas import tpu as pltpu
from jax.sharding import Mesh
from jax.sharding import PartitionSpec as P

GRID = 512
ROWS = 32
PEERS = 16
RECV = 64
GAIN = 3.0
f32 = jnp.float32
bf16 = jnp.bfloat16


def dft_tables():
    k = np.arange(GRID, dtype=np.int64)
    angle = ((k[:, None] * k[None, :]) % GRID).astype(np.float32) * np.float32(2.0 * math.pi / GRID)
    scale = np.float32(1.0 / math.sqrt(GRID))
    both = np.stack([np.cos(angle) * scale, np.sin(angle) * scale])
    return both.astype(ml_dtypes.bfloat16)


def mm(a, b):
    return jnp.dot(a, b, preferred_element_type=f32)


def mm_nt(a, b):
    return lax.dot_general(a, b, (((1,), (1,)), ((), ())), preferred_element_type=f32)


def swap_groups(x):
    lane = lax.broadcasted_iota(jnp.int32, x[0].shape, 1)
    low = lane < 64
    even = (lane & 32) == 0
    a0 = jnp.where(low, x[0], pltpu.roll(x[2], 64, 1))
    a2 = jnp.where(low, pltpu.roll(x[0], 64, 1), x[2])
    a1 = jnp.where(low, x[1], pltpu.roll(x[3], 64, 1))
    a3 = jnp.where(low, pltpu.roll(x[1], 64, 1), x[3])
    y0 = jnp.where(even, a0, pltpu.roll(a1, 32, 1))
    y1 = jnp.where(even, pltpu.roll(a0, 96, 1), a1)
    y2 = jnp.where(even, a2, pltpu.roll(a3, 32, 1))
    y3 = jnp.where(even, pltpu.roll(a2, 96, 1), a3)
    return [y0, y1, y2, y3]


def lines_of(tiles):
    parts = [[], [], [], []]
    for g in range(4):
        swapped = swap_groups([tiles[4 * g + i, 0:ROWS, :].astype(f32) for i in range(4)])
        for j in range(4):
            parts[j].append(swapped[j])
    return jnp.concatenate([jnp.concatenate(p, axis=1) for p in parts], axis=0).astype(bf16)


def store_tiles(out, re, im):
    quarter = [re[0:ROWS], re[ROWS:], im[0:ROWS], im[ROWS:]]
    for g in range(4):
        swapped = swap_groups([q[:, 128 * g : 128 * g + 128] for q in quarter])
        for j in range(4):
            out[4 * g + j] = swapped[j].astype(bf16)


def inv_lines(lines, table):
    a = mm(lines, table[0])
    b = mm(lines, table[1])
    return a[0:64] - b[64:128], a[64:128] + b[0:64]


def fwd_lines(re, im, table):
    both = jnp.concatenate([re, im], axis=0).astype(bf16)
    a = mm(both, table[0])
    b = mm(both, table[1])
    return a[0:64] + b[64:128], a[64:128] - b[0:64]


def times(cre, cim, ure, uim):
    return cre * ure - cim * uim, cre * uim + cim * ure


def inv_spectrum(hre, him, table):
    straight = jnp.concatenate([hre, him], axis=0).astype(bf16)
    crossed = jnp.concatenate([-him, hre], axis=0).astype(bf16)
    return mm_nt(table[0], straight) + mm_nt(table[1], crossed)


def couple(kernel, fre, fim):
    hre = []
    him = []
    for lo in range(2):
        sre = None
        sim = None
        for li in range(2):
            kre = kernel[0, lo, li].astype(f32)
            kim = kernel[1, lo, li].astype(f32)
            vre = fre[ROWS * li : ROWS * li + ROWS]
            vim = fim[ROWS * li : ROWS * li + ROWS]
            pre, pim = times(kre, kim, vre, vim)
            sre = pre if sre is None else sre + pre
            sim = pim if sim is None else sim + pim
        hre.append(sre)
        him.append(sim)
    return jnp.concatenate(hre, axis=0), jnp.concatenate(him, axis=0)


def source_body(spot, kernel, table, out):
    x0 = spot[0]
    y0 = spot[1]
    first = spot[2]
    step = 2.0 * math.pi / GRID
    kx = lax.broadcasted_iota(jnp.int32, (8, GRID), 1)
    ax = ((kx * x0) & (GRID - 1)).astype(f32) * step
    ky = lax.broadcasted_iota(jnp.int32, (ROWS, 128), 0) + first
    ay = ((ky * y0) & (GRID - 1)).astype(f32) * step
    xre = jnp.cos(ax)[0:1]
    xim = -jnp.sin(ax)[0:1]
    yre = jnp.cos(ay)[:, 0:1]
    yim = -jnp.sin(ay)[:, 0:1]
    qre = GAIN * (yre * xre - yim * xim)
    qim = GAIN * (yre * xim + yim * xre)
    zre = []
    zim = []
    for lo in range(2):
        a, b = times(kernel[0, lo, 0].astype(f32), kernel[1, lo, 0].astype(f32), qre, qim)
        zre.append(a)
        zim.append(b)
    field = inv_spectrum(jnp.concatenate(zre, axis=0), jnp.concatenate(zim, axis=0), table)
    out[...] = field.astype(bf16).reshape(PEERS, ROWS, 128)


def first_line_body(tiles, contrast, table, incident, out):
    ure, uim = inv_lines(lines_of(tiles), table)
    incident[0:64] = ure
    incident[64:128] = uim
    vre, vim = times(contrast[0:64], contrast[64:128], ure, uim)
    wre, wim = fwd_lines(vre, vim, table)
    store_tiles(out, wre, wim)


def line_body(tiles, contrast, incident, table, out):
    dre, dim = inv_lines(lines_of(tiles), table)
    ure = incident[0:64] + dre
    uim = incident[64:128] + dim
    vre, vim = times(contrast[0:64], contrast[64:128], ure, uim)
    wre, wim = fwd_lines(vre, vim, table)
    store_tiles(out, wre, wim)


def spectral(tiles, kernel, table):
    turned = tiles[...].reshape(GRID, 128).astype(f32).T.astype(bf16)
    a = mm(turned, table[0])
    b = mm(turned, table[1])
    fre = a[0:64] + b[64:128]
    fim = a[64:128] - b[0:64]
    hre, him = couple(kernel, fre, fim)
    return inv_spectrum(hre, him, table).astype(bf16)


def spectral_body(tiles, kernel, table, out):
    out[...] = spectral(tiles, kernel, table).reshape(PEERS, ROWS, 128)


def picks(column):
    where = lax.broadcasted_iota(jnp.int32, (RECV, GRID), 1)
    return jnp.where(where == column, 1.0, 0.0).astype(bf16)


def own_tables(spot, table):
    first = pl.multiple_of(spot[2], ROWS)
    return table[0, pl.ds(first, ROWS), :], table[1, pl.ds(first, ROWS), :]


def sampled_body(spot, tiles, kernel, table, source, columns, out):
    field = spectral(tiles, kernel, table)
    out[:, 0:ROWS, :] = field.reshape(PEERS, ROWS, 128)
    at_x = picks(columns[:, 0:1])
    at_y = picks(columns[:, 1:2])
    taken = mm(at_x, field) + mm(at_x, source[...].reshape(GRID, 128))
    cown, sown = own_tables(spot, table)
    zero = jnp.zeros((ROWS, GRID), bf16)
    phase_re = mm_nt(at_y, jnp.concatenate([cown, zero, -sown, zero], axis=0))
    phase_im = mm_nt(at_y, jnp.concatenate([sown, zero, cown, zero], axis=0))
    terms = jnp.concatenate([taken * phase_re, taken * phase_im], axis=0)
    total = jnp.sum(terms.T, axis=0, keepdims=True)
    high = total.astype(bf16).astype(f32)
    low = total - high
    row = lax.broadcasted_iota(jnp.int32, (16, 128), 0)
    extra = jnp.where(row == 0, high, jnp.where(row == 1, low, 0.0)).astype(bf16)
    for d in range(PEERS):
        out[d, ROWS : ROWS + 16, :] = extra


def back_body(spot, tiles, kernel, table, measured, columns, out):
    sums = jnp.zeros((16, 128), f32)
    for s in range(PEERS):
        sums = sums + tiles[s, ROWS : ROWS + 16, :].astype(f32)
    misfit = sums[0:1] + sums[1:2] - measured[...]
    mre = misfit[:, 0:RECV]
    mim = misfit[:, RECV : 2 * RECV]
    at_x = picks(columns[:, 0:1])
    at_y = picks(columns[:, 1:2])
    cown, sown = own_tables(spot, table)
    yre = mm_nt(cown, at_y)
    yim = mm_nt(sown, at_y)
    mixed_re = mre * yre + mim * yim
    mixed_im = mim * yre - mre * yim
    mixed = jnp.concatenate([mixed_re, mixed_im], axis=0).astype(bf16)
    a = mm(mixed, mm(at_x, table[0]).astype(bf16))
    b = mm(mixed, mm(at_x, table[1]).astype(bf16))
    bre = (a[0:ROWS] + b[ROWS : 2 * ROWS]) * float(GRID)
    bim = (a[ROWS : 2 * ROWS] - b[0:ROWS]) * float(GRID)
    yre = []
    yim = []
    for l in range(2):
        kre = kernel[0, 0, l].astype(f32)
        kim = kernel[1, 0, l].astype(f32)
        yre.append(kre * bre + kim * bim)
        yim.append(kre * bim - kim * bre)
    field = inv_spectrum(jnp.concatenate(yre, axis=0), jnp.concatenate(yim, axis=0), table)
    out[...] = field.astype(bf16).reshape(PEERS, ROWS, 128)


def field_body(tiles, incident, table, out):
    dre, dim = inv_lines(lines_of(tiles), table)
    out[0:64] = incident[0:64] + dre
    out[64:128] = incident[64:128] + dim


def gradient_body(tiles, wave, table, out):
    bre, bim = inv_lines(lines_of(tiles), table)
    ure = wave[0:64]
    uim = wave[64:128]
    gre = (ure * bre + uim * bim).astype(bf16)
    gim = (ure * bim - uim * bre).astype(bf16)
    for s in range(PEERS):
        row = ROWS * (s // 4)
        part = gre if row < 64 else gim
        out[s] = part[row % 64 : row % 64 + ROWS, 128 * (s % 4) : 128 * (s % 4) + 128]


def share_body(arrived, out):
    total = jnp.zeros((ROWS, 128), f32)
    for s in range(PEERS):
        total = total + arrived[s].astype(f32)
    total = total.astype(bf16)
    for d in range(2 * PEERS):
        out[d] = total


def update_body(shares, contrast, wave, table, updated, out):
    freqs = 2.0 * PEERS
    for s in range(PEERS):
        z = s // 2
        core = s % 2
        row = ROWS * (s // 4)
        lane = 128 * (s % 4)
        total = shares[4 * z + core].astype(f32) + shares[4 * z + 2 + core].astype(f32)
        updated[row : row + ROWS, lane : lane + 128] = (
            contrast[row : row + ROWS, lane : lane + 128] - total / freqs
        )
    vre, vim = times(updated[0:64], updated[64:128], wave[0:64], wave[64:128])
    wre, wim = fwd_lines(vre, vim, table)
    store_tiles(out, wre, wim)


TILES = ((PEERS, ROWS, 128), bf16)
LINES = ((128, GRID), f32)
IN_VMEM = pl.BlockSpec(memory_space=pltpu.VMEM)
IN_SMEM = pl.BlockSpec(memory_space=pltpu.SMEM)


def run(body, outs, *args, scalars=0):
    many = isinstance(outs, list)
    shapes = [jax.ShapeDtypeStruct(*o) for o in (outs if many else [outs])]
    result = pl.pallas_call(
        body,
        out_shape=shapes if many else shapes[0],
        in_specs=[IN_SMEM if i < scalars else IN_VMEM for i in range(len(args))],
        out_specs=[IN_VMEM] * len(shapes) if many else IN_VMEM,
        compiler_params=pltpu.CompilerParams(vmem_limit_bytes=40 * 1024 * 1024),
    )(*args)
    return result


def exchange(blocks, axes):
    return lax.all_to_all(blocks, axes, split_axis=0, concat_axis=0, tiled=True)


def by_part_layer(field):
    return field.transpose(0, 2, 1, 3).reshape(128, GRID)


def by_row(lines):
    return lines.reshape(2, 2, ROWS, GRID).transpose(0, 2, 1, 3)


def local(contrast, green_kernel, source_pos, receiver_pos, measured):
    table = jnp.asarray(dft_tables())
    kernel = green_kernel[0]
    first = lax.axis_index("plane") * ROWS
    spot = jnp.concatenate([source_pos[0].astype(jnp.int32), first.astype(jnp.int32)[None]])
    columns = receiver_pos[0].T
    observed = measured.reshape(1, 2 * RECV)
    lines = by_part_layer(contrast)

    source = run(source_body, TILES, spot, kernel, table, scalars=1)
    arrived = exchange(source, "plane")
    incident, sent = run(first_line_body, [LINES, TILES], arrived, lines, table)
    arrived = exchange(sent, "plane")
    sent = run(spectral_body, TILES, arrived, kernel, table)
    arrived = exchange(sent, "plane")
    sent = run(line_body, TILES, arrived, lines, incident, table)
    arrived = exchange(sent, "plane")
    wide = ((PEERS, ROWS + 16, 128), bf16)
    sent = run(sampled_body, wide, spot, arrived, kernel, table, source, columns, scalars=1)
    arrived = exchange(sent, "plane")
    sent = run(back_body, TILES, spot, arrived, kernel, table, observed, columns, scalars=1)
    wave = run(field_body, LINES, arrived, incident, table)
    arrived = exchange(sent, "plane")
    sent = run(gradient_body, TILES, arrived, wave, table)
    arrived = exchange(sent, ("z", "core"))
    sent = run(share_body, ((2 * PEERS, ROWS, 128), bf16), arrived)
    arrived = exchange(sent, ("z", "yh", "core"))
    updated, sent = run(update_body, [LINES, TILES], arrived, lines, wave, table)
    arrived = exchange(sent, "plane")
    sent = run(spectral_body, TILES, arrived, kernel, table)
    arrived = exchange(sent, "plane")
    field = run(field_body, LINES, arrived, incident, table)
    return by_row(updated), by_row(field)[None]


def solution(mesh):
    freqs = mesh.shape["freq"]
    split = Mesh(
        mesh.devices.reshape(freqs // 4, 2, 2, mesh.shape["plane"]), ("z", "yh", "core", "plane")
    )
    freq = ("z", "yh", "core")
    return jax.shard_map(
        local,
        mesh=split,
        in_specs=(
            P(None, "plane", None, None),
            P(freq, None, None, None, "plane", None),
            P(freq, None),
            P(freq, None, None),
            P(freq, None, None),
        ),
        out_specs=(P(None, "plane", None, None), P(freq, None, "plane", None, None)),
        check_vma=False,
    )
```

time: 231 us -> 160 us (0.69)
  local copies, waits for them, and re-layouts: 50.4 us -> 5.55 us
  blocking collectives: 55.8 us -> 74.2 us
  starting transfers between devices: 45.4 us -> 28.5 us
  waiting for transfers between devices: 50.7 us -> 36.5 us
  matrix products: 14.2 us -> 0 us
  Pallas kernels: 0 us -> 13.8 us
  other arithmetic: 11 us -> 0.07 us
    unnamed x78 -> x16, local copies, waits for them, and re-layouts: 23.3 us -> 3.51 us
    all_to_all x4 -> x5, blocking collectives: 55.8 us -> 74.2 us  [exchange(): return lax.all_to_all(blocks, axes, split_axis=0, concat_axis=0, tiled=True)]
    all_to_all x7 -> x5, starting transfers between devices: 45.4 us -> 28.5 us  [exchange(): return lax.all_to_all(blocks, axes, split_axis=0, concat_axis=0, tiled=True)]
    dot_general x21 -> x0, matrix products: 14.2 us -> none  [the longest x3 4.52 us: forward(): jnp.einsum('cxq,xk->cqk', merged, dft_table, preferred_element_type=jnp.f...]
    all_to_all x7 -> x5, waiting for transfers between devices: 50.7 us -> 36.5 us  [exchange(): return lax.all_to_all(blocks, axes, split_axis=0, concat_axis=0, tiled=True)]
    pallas_call x0 -> x12, Pallas kernels: none -> 13.8 us  [run(): pl.pallas_call(body, out_shape=shapes if many else shapes[0], in_specs=[I...]
    dot_general x8 -> x0, local copies, waits for them, and re-layouts: 7.65 us -> none  [inverse(): jnp.dot(arrived.reshape(2 * row_count * layer_count, grid_size), dft_tabl...]
    another operation x36 -> x0, other arithmetic: 6.62 us -> none
  transfers between devices with their start and end apart: 7 -> 5, of which waited for: 7 -> 5; matrix products, arithmetic and copies ran while one was open for 3% -> 1% of each run, Pallas kernels for 0% -> 0%
where the time goes in v1:
time: 160 us; the launch traced here: 159 us
  blocking collectives  74.2 us (46%)
  waiting for transfers between devices  36.5 us (23%)
  starting transfers between devices  28.5 us (18%)
  Pallas kernels  13.8 us (9%)
  local copies, waits for them, and re-layouts  5.55 us (3%)
    all_to_all x5, blocking collectives, exchange(): return lax.all_to_all(blocks, axes, split_axis=0, concat_axis=0, tiled=True)  74.2 us
    all_to_all x5, waiting for transfers between devices, exchange(): return lax.all_to_all(blocks, axes, split_axis=0, concat_axis=0, tiled=True)  36.5 us
    all_to_all x5, starting transfers between devices, exchange(): return lax.all_to_all(blocks, axes, split_axis=0, concat_axis=0, tiled=True)  28.5 us
    pallas_call x12, Pallas kernels, run(): pl.pallas_call(body, out_shape=shapes if many else shapes[0], in_specs=[I...  13.8 us
    unnamed x16, local copies, waits for them, and re-layouts  3.51 us
  transfers between devices with their start and end apart: 5, of which 5 were waited for; matrix products, arithmetic and copies ran while one was open for 1% of the time, Pallas kernels for 0%

profile of v1, /device:TPU:2, one launch (start us, length us, event | category | flops | bytes accessed | tf_op | source)
XLA Modules:
  0.0 159.3 jit_solution(18345071608054064786)
XLA Ops:
  1.4 1.2 copy-done
  2.6 0.9 copy-done.2
  3.5 1.8 %shard_map.77.source = bf16[16,32,128]{2,1,0:T(8,128)(2,1)} custom-call(s32[3]{0:T(128)S(1)} %pad_add_fusion.spot, bf16[2,2,2,32,512]{4,3,2,1,0:T(8,128)(2,1)S(1)} %bitcast.17, bf16[2,512,512]{2,1,0:T(8,128)(2,1)S(1)} %copy-done), custom_call_target="tpu_custom_call" | custom-call | tf_op jit(solution)/shard_map/pallas_call | solution.py:281
  5.3 9.3 %all-to-all-start = ((bf16[16,32,128]{2,1,0:T(8,128)(2,1)}), bf16[16,32,128]{2,1,0:T(8,128)(2,1)S(1)}, u32[]{:S(2)}, u32[]{:S(2)}) async-start(bf16[16,32,128]{2,1,0:T(8,128)(2,1)} %shard_map.77.source), calls=%async_computation | async-start | bytes 262144 | tf_op jit(solution)/shard_map/all_to_all | solution.py:292
  14.7 7.6 %all-to-all-done.tiles = bf16[16,32,128]{2,1,0:T(8,128)(2,1)S(1)} async-done(((bf16[16,32,128]{2,1,0:T(8,128)(2,1)}), bf16[16,32,128]{2,1,0:T(8,128)(2,1)S(1)}, u32[]{:S(2)}, u32[]{:S(2)}) %all-to-all-start) | async-done | bytes 131104 | tf_op jit(solution)/shard_map/all_to_all | solution.py:292
  22.3 0.9 shard_map.78
  23.2 11.6 %all_to_all.50.tiles = bf16[16,32,128]{2,1,0:T(8,128)(2,1)S(1)} all-to-all(bf16[16,32,128]{2,1,0:T(8,128)(2,1)S(1)} %get-tuple-element.6), channel_id=1, replica_groups=mesh['z'=8,'yh'=2,'core'=2,'plane'=16] {'plane'}, dimensions={0} | all-to-all | bytes 262144 | tf_op jit(solution)/shard_map/all_to_all | solution.py:292
  35.8 11.5 %all_to_all.51.tiles = bf16[16,32,128]{2,1,0:T(8,128)(2,1)S(1)} all-to-all(bf16[16,32,128]{2,1,0:T(8,128)(2,1)S(1)} %shard_map.79), channel_id=1, replica_groups=mesh['z'=8,'yh'=2,'core'=2,'plane'=16] {'plane'}, dimensions={0} | all-to-all | bytes 262144 | tf_op jit(solution)/shard_map/all_to_all | solution.py:292
  47.3 1.5 shard_map.80
  48.8 4.8 %all-to-all-start.3 = ((bf16[16,32,128]{2,1,0:T(8,128)(2,1)}), bf16[16,32,128]{2,1,0:T(8,128)(2,1)S(1)}, u32[]{:S(2)}, u32[]{:S(2)}) async-start(bf16[16,32,128]{2,1,0:T(8,128)(2,1)} %shard_map.80), calls=%async_computation.3 | async-start | bytes 262144 | tf_op jit(solution)/shard_map/all_to_all | solution.py:292
  54.4 6.9 %all-to-all-done.3.tiles = bf16[16,32,128]{2,1,0:T(8,128)(2,1)S(1)} async-done(((bf16[16,32,128]{2,1,0:T(8,128)(2,1)}), bf16[16,32,128]{2,1,0:T(8,128)(2,1)S(1)}, u32[]{:S(2)}, u32[]{:S(2)}) %all-to-all-start.3) | async-done | bytes 131104 | tf_op jit(solution)/shard_map/all_to_all | solution.py:292
  61.2 2.8 %shard_map.81 = bf16[16,48,128]{2,1,0:T(8,128)(2,1)} custom-call(s32[3]{0:T(128)S(1)} %pad_add_fusion.spot, bf16[16,32,128]{2,1,0:T(8,128)(2,1)S(1)} %all-to-all-done.3.tiles, bf16[2,2,2,32,512]{4,3,2,1,0:T(8,128)(2,1)S(1)} %bitcast.19, bf16[2,512,512]{2,1,0:T(8,128)(2,1)S(1)} %copy-done.1, bf16[16,32,128]{2,1,0:T(8,128)(2,1)} %shard_map.77.source, ...), custom_call_target="tpu_custom_call" | custom-call | tf_op jit(solution)/shard_map/pallas_call | solution.py:281
  64.1 4.9 %all-to-all-start.4 = ((bf16[16,48,128]{2,1,0:T(8,128)(2,1)}), bf16[16,48,128]{2,1,0:T(8,128)(2,1)S(1)}, u32[]{:S(2)}, u32[]{:S(2)}) async-start(bf16[16,48,128]{2,1,0:T(8,128)(2,1)} %shard_map.81), calls=%async_computation.4 | async-start | bytes 393216 | tf_op jit(solution)/shard_map/all_to_all | solution.py:292
  69.1 8.1 %all-to-all-done.4.tiles = bf16[16,48,128]{2,1,0:T(8,128)(2,1)S(1)} async-done(((bf16[16,48,128]{2,1,0:T(8,128)(2,1)}), bf16[16,48,128]{2,1,0:T(8,128)(2,1)S(1)}, u32[]{:S(2)}, u32[]{:S(2)}) %all-to-all-start.4) | async-done | bytes 196640 | tf_op jit(solution)/shard_map/all_to_all | solution.py:292
  77.2 2.4 %shard_map.82 = bf16[16,32,128]{2,1,0:T(8,128)(2,1)} custom-call(s32[3]{0:T(128)S(1)} %pad_add_fusion.spot, bf16[16,48,128]{2,1,0:T(8,128)(2,1)S(1)} %all-to-all-done.4.tiles, bf16[2,2,2,32,512]{4,3,2,1,0:T(8,128)(2,1)S(1)} %bitcast.20, bf16[2,512,512]{2,1,0:T(8,128)(2,1)S(1)} %copy-done.1, f32[1,128]{1,0:T(1,128)S(1)} %reshape.17.measured, s32[64,2]{1,0:T(8,128)S(1)} %bitcast.27), custom_call_target="tpu_custom_call" | custom-call | tf_op jit(solution)/shard_map/pallas_call | solution.py:281
  79.6 4.8 %all-to-all-start.5 = ((bf16[16,32,128]{2,1,0:T(8,128)(2,1)}), bf16[16,32,128]{2,1,0:T(8,128)(2,1)S(1)}, u32[]{:S(2)}, u32[]{:S(2)}) async-start(bf16[16,32,128]{2,1,0:T(8,128)(2,1)} %shard_map.82), calls=%async_computation.5 | async-start | bytes 262144 | tf_op jit(solution)/shard_map/all_to_all | solution.py:292
  84.8 7.2 %all-to-all-done.5.tiles = bf16[16,32,128]{2,1,0:T(8,128)(2,1)S(1)} async-done(((bf16[16,32,128]{2,1,0:T(8,128)(2,1)}), bf16[16,32,128]{2,1,0:T(8,128)(2,1)S(1)}, u32[]{:S(2)}, u32[]{:S(2)}) %all-to-all-start.5) | async-done | bytes 131104 | tf_op jit(solution)/shard_map/all_to_all | solution.py:292
  92.5 17.6 %all_to_all.52.arrived = bf16[16,32,128]{2,1,0:T(8,128)(2,1)S(1)} all-to-all(bf16[16,32,128]{2,1,0:T(8,128)(2,1)S(1)} %shard_map.84), channel_id=1, replica_groups=mesh['z'=8,'yh'=2,'core'=2,'plane'=16] {'z','core'}, dimensions={0} | all-to-all | bytes 262144 | tf_op jit(solution)/shard_map/all_to_all | solution.py:292
  110.1 19.8 %all_to_all.53.shares = bf16[32,32,128]{2,1,0:T(8,128)(2,1)S(1)} all-to-all(bf16[32,32,128]{2,1,0:T(8,128)(2,1)S(1)} %shard_map.85), channel_id=1, replica_groups=mesh['z'=8,'yh'=2,'core'=2,'plane'=16] {'z','yh','core'}, dimensions={0} | all-to-all | bytes 524288 | tf_op jit(solution)/shard_map/all_to_all | solution.py:292
  130.4 13.6 %all_to_all.54.tiles = bf16[16,32,128]{2,1,0:T(8,128)(2,1)S(1)} all-to-all(bf16[16,32,128]{2,1,0:T(8,128)(2,1)S(1)} %get-tuple-element.9), channel_id=1, replica_groups=mesh['z'=8,'yh'=2,'core'=2,'plane'=16] {'plane'}, dimensions={0} | all-to-all | bytes 262144 | tf_op jit(solution)/shard_map/all_to_all | solution.py:292
  144.0 1.5 shard_map.87
  145.5 4.8 %all-to-all-start.9 = ((bf16[16,32,128]{2,1,0:T(8,128)(2,1)}), bf16[16,32,128]{2,1,0:T(8,128)(2,1)S(1)}, u32[]{:S(2)}, u32[]{:S(2)}) async-start(bf16[16,32,128]{2,1,0:T(8,128)(2,1)} %shard_map.87), calls=%async_computation.9 | async-start | bytes 262144 | tf_op jit(solution)/shard_map/all_to_all | solution.py:292
  151.2 6.7 %all-to-all-done.9.tiles = bf16[16,32,128]{2,1,0:T(8,128)(2,1)S(1)} async-done(((bf16[16,32,128]{2,1,0:T(8,128)(2,1)}), bf16[16,32,128]{2,1,0:T(8,128)(2,1)S(1)}, u32[]{:S(2)}, u32[]{:S(2)}) %all-to-all-start.9) | async-done | bytes 131104 | tf_op jit(solution)/shard_map/all_to_all | solution.py:292
  158.4 0.9 copy.14
  (25 shorter events, 5.3 us)
Async XLA Ops:
  0.6 0.7 copy-start.7
  1.4 1.2 copy-start
  2.6 0.9 copy-start.2
  3.5 18.8 %copy-start.1 = (bf16[2,512,512]{2,1,0:T(8,128)(2,1)S(1)}, bf16[2,512,512]{2,1,0:T(8,128)(2,1)}, u32[]{:S(2)}) copy-start(bf16[2,512,512]{2,1,0:T(8,128)(2,1)} %constant.8.clone.table) | copy-start | bytes 3145732
  5.3 9.3 %copy-start.4 = (f32[2,32,2,512]{3,2,1,0:T(2,128)S(1)}, f32[2,32,2,512]{3,2,1,0:T(2,128)}, u32[]{:S(2)}) copy-start(f32[2,32,2,512]{3,2,1,0:T(2,128)} %param.6) | copy-start | bytes 786436
  5.3 17.0 %all-to-all-start = ((bf16[16,32,128]{2,1,0:T(8,128)(2,1)}), bf16[16,32,128]{2,1,0:T(8,128)(2,1)S(1)}, u32[]{:S(2)}, u32[]{:S(2)}) async-start(bf16[16,32,128]{2,1,0:T(8,128)(2,1)} %shard_map.77.source), calls=%async_computation | async-start | bytes 262144 | tf_op jit(solution)/shard_map/all_to_all | solution.py:292
  23.2 11.7 %copy-start.3 = (bf16[1,2,2,2,32,512]{5,4,3,2,1,0:T(8,128)(2,1)S(1)}, bf16[1,2,2,2,32,512]{5,4,3,2,1,0:T(8,128)(2,1)}, u32[]{:S(2)}) copy-start(bf16[1,2,2,2,32,512]{5,4,3,2,1,0:T(8,128)(2,1)} %param.7) | copy-start | bytes 786436
  48.8 12.4 %all-to-all-start.3 = ((bf16[16,32,128]{2,1,0:T(8,128)(2,1)}), bf16[16,32,128]{2,1,0:T(8,128)(2,1)S(1)}, u32[]{:S(2)}, u32[]{:S(2)}) async-start(bf16[16,32,128]{2,1,0:T(8,128)(2,1)} %shard_map.80), calls=%async_computation.3 | async-start | bytes 262144 | tf_op jit(solution)/shard_map/all_to_all | solution.py:292
  53.6 0.7 copy-start.5
  64.1 4.9 %copy-start.6 = (f32[1,2,64]{2,1,0:T(2,128)S(1)}, f32[1,2,64]{2,1,0:T(2,128)}, u32[]{:S(2)}) copy-start(f32[1,2,64]{2,1,0:T(2,128)} %param.10) | copy-start | bytes 1540
  64.1 13.1 %all-to-all-start.4 = ((bf16[16,48,128]{2,1,0:T(8,128)(2,1)}), bf16[16,48,128]{2,1,0:T(8,128)(2,1)S(1)}, u32[]{:S(2)}, u32[]{:S(2)}) async-start(bf16[16,48,128]{2,1,0:T(8,128)(2,1)} %shard_map.81), calls=%async_computation.4 | async-start | bytes 393216 | tf_op jit(solution)/shard_map/all_to_all | solution.py:292
  79.6 12.4 %all-to-all-start.5 = ((bf16[16,32,128]{2,1,0:T(8,128)(2,1)}), bf16[16,32,128]{2,1,0:T(8,128)(2,1)S(1)}, u32[]{:S(2)}, u32[]{:S(2)}) async-start(bf16[16,32,128]{2,1,0:T(8,128)(2,1)} %shard_map.82), calls=%async_computation.5 | async-start | bytes 262144 | tf_op jit(solution)/shard_map/all_to_all | solution.py:292
  145.5 12.4 %all-to-all-start.9 = ((bf16[16,32,128]{2,1,0:T(8,128)(2,1)}), bf16[16,32,128]{2,1,0:T(8,128)(2,1)S(1)}, u32[]{:S(2)}, u32[]{:S(2)}) async-start(bf16[16,32,128]{2,1,0:T(8,128)(2,1)} %shard_map.87), calls=%async_computation.9 | async-start | bytes 262144 | tf_op jit(solution)/shard_map/all_to_all | solution.py:292

commit v2 on v1

v2 whole, which is shorter than its diff:
```python
import math

import jax
import jax.numpy as jnp
import ml_dtypes
import numpy as np
from jax import lax
from jax.experimental import pallas as pl
from jax.experimental.pallas import tpu as pltpu
from jax.sharding import Mesh
from jax.sharding import PartitionSpec as P

GRID = 512
ROWS = 32
PEERS = 16
RECV = 64
GAIN = 3.0
f32 = jnp.float32
bf16 = jnp.bfloat16


def dft_tables():
    k = np.arange(GRID, dtype=np.int64)
    angle = ((k[:, None] * k[None, :]) % GRID).astype(np.float32) * np.float32(2.0 * math.pi / GRID)
    scale = np.float32(1.0 / math.sqrt(GRID))
    both = np.stack([np.cos(angle) * scale, np.sin(angle) * scale])
    return both.astype(ml_dtypes.bfloat16)


def mm(a, b):
    return jnp.dot(a, b, preferred_element_type=f32)


def mm_nt(a, b):
    return lax.dot_general(a, b, (((1,), (1,)), ((), ())), preferred_element_type=f32)


def swap_groups(x):
    lane = lax.broadcasted_iota(jnp.int32, x[0].shape, 1)
    low = lane < 64
    even = (lane & 32) == 0
    a0 = jnp.where(low, x[0], pltpu.roll(x[2], 64, 1))
    a2 = jnp.where(low, pltpu.roll(x[0], 64, 1), x[2])
    a1 = jnp.where(low, x[1], pltpu.roll(x[3], 64, 1))
    a3 = jnp.where(low, pltpu.roll(x[1], 64, 1), x[3])
    y0 = jnp.where(even, a0, pltpu.roll(a1, 32, 1))
    y1 = jnp.where(even, pltpu.roll(a0, 96, 1), a1)
    y2 = jnp.where(even, a2, pltpu.roll(a3, 32, 1))
    y3 = jnp.where(even, pltpu.roll(a2, 96, 1), a3)
    return [y0, y1, y2, y3]


def lines_of(tiles):
    parts = [[], [], [], []]
    for g in range(4):
        swapped = swap_groups([tiles[4 * g + i, 0:ROWS, :].astype(f32) for i in range(4)])
        for j in range(4):
            parts[j].append(swapped[j])
    return jnp.concatenate([jnp.concatenate(p, axis=1) for p in parts], axis=0).astype(bf16)


def store_tiles(out, re, im):
    quarter = [re[0:ROWS], re[ROWS:], im[0:ROWS], im[ROWS:]]
    for g in range(4):
        swapped = swap_groups([q[:, 128 * g : 128 * g + 128] for q in quarter])
        for j in range(4):
            out[4 * g + j] = swapped[j].astype(bf16)


def inv_lines(lines, table):
    a = mm(lines, table[0])
    b = mm(lines, table[1])
    return a[0:64] - b[64:128], a[64:128] + b[0:64]


def fwd_lines(re, im, table):
    both = jnp.concatenate([re, im], axis=0).astype(bf16)
    a = mm(both, table[0])
    b = mm(both, table[1])
    return a[0:64] + b[64:128], a[64:128] - b[0:64]


def times(cre, cim, ure, uim):
    return cre * ure - cim * uim, cre * uim + cim * ure


def inv_spectrum(hre, him, table):
    straight = jnp.concatenate([hre, him], axis=0).astype(bf16)
    crossed = jnp.concatenate([-him, hre], axis=0).astype(bf16)
    return mm_nt(table[0], straight) + mm_nt(table[1], crossed)


def couple(kernel, fre, fim):
    hre = []
    him = []
    for lo in range(2):
        sre = None
        sim = None
        for li in range(2):
            kre = kernel[0, lo, li].astype(f32)
            kim = kernel[1, lo, li].astype(f32)
            vre = fre[ROWS * li : ROWS * li + ROWS]
            vim = fim[ROWS * li : ROWS * li + ROWS]
            pre, pim = times(kre, kim, vre, vim)
            sre = pre if sre is None else sre + pre
            sim = pim if sim is None else sim + pim
        hre.append(sre)
        him.append(sim)
    return jnp.concatenate(hre, axis=0), jnp.concatenate(him, axis=0)


def source_body(spot_hbm, first, kernel_hbm, table_hbm, out, spectrum, kernel, table, spot, sems):
    copies = []
    where = pltpu.make_async_copy(spot_hbm, spot, sems.at[4])
    where.start()
    for part in range(2):
        copies.append(
            pltpu.make_async_copy(
                kernel_hbm.at[part, :, 0], kernel.at[part], sems.at[part]
            )
        )
        copies.append(
            pltpu.make_async_copy(table_hbm.at[part], table.at[part], sems.at[2 + part])
        )
    for copy in (copies[0], copies[2], copies[1], copies[3]):
        copy.start()
    where.wait()
    x0 = spot[0, 0]
    y0 = spot[0, 1]
    step = 2.0 * math.pi / GRID
    kx = lax.broadcasted_iota(jnp.int32, (8, GRID), 1)
    ax = ((kx * x0) & (GRID - 1)).astype(f32) * step
    ky = lax.broadcasted_iota(jnp.int32, (ROWS, 128), 0) + first[0]
    ay = ((ky * y0) & (GRID - 1)).astype(f32) * step
    xre = jnp.cos(ax)[0:1]
    xim = -jnp.sin(ax)[0:1]
    yre = jnp.cos(ay)[:, 0:1]
    yim = -jnp.sin(ay)[:, 0:1]
    qre = GAIN * (yre * xre - yim * xim)
    qim = GAIN * (yre * xim + yim * xre)
    copies[0].wait()
    copies[2].wait()
    zre = []
    zim = []
    for lo in range(2):
        a, b = times(kernel[0, lo].astype(f32), kernel[1, lo].astype(f32), qre, qim)
        zre.append(a)
        zim.append(b)
    zre = jnp.concatenate(zre, axis=0)
    zim = jnp.concatenate(zim, axis=0)
    straight = jnp.concatenate([zre, zim], axis=0).astype(bf16)
    crossed = jnp.concatenate([-zim, zre], axis=0).astype(bf16)
    spectrum[...] = straight
    copies[1].wait()
    field = mm_nt(table[0], straight)
    copies[3].wait()
    field = field + mm_nt(table[1], crossed)
    out[...] = field.astype(bf16).reshape(PEERS, ROWS, 128)


def by_part_layer(field, part):
    return jnp.concatenate([field[part, :, 0, :], field[part, :, 1, :]], axis=0)


def first_line_body(tiles, contrast, table, incident, lines, out):
    ure, uim = inv_lines(lines_of(tiles), table)
    incident[0:64] = ure
    incident[64:128] = uim
    cre = by_part_layer(contrast, 0)
    cim = by_part_layer(contrast, 1)
    lines[0:64] = cre
    lines[64:128] = cim
    vre, vim = times(cre, cim, ure, uim)
    wre, wim = fwd_lines(vre, vim, table)
    store_tiles(out, wre, wim)


def line_body(tiles, contrast, incident, table, out):
    dre, dim = inv_lines(lines_of(tiles), table)
    ure = incident[0:64] + dre
    uim = incident[64:128] + dim
    vre, vim = times(contrast[0:64], contrast[64:128], ure, uim)
    wre, wim = fwd_lines(vre, vim, table)
    store_tiles(out, wre, wim)


def coupled(tiles, kernel, table):
    turned = tiles[...].reshape(GRID, 128).astype(f32).T.astype(bf16)
    a = mm(turned, table[0])
    b = mm(turned, table[1])
    fre = a[0:64] + b[64:128]
    fim = a[64:128] - b[0:64]
    return couple(kernel, fre, fim)


def spectral_body(tiles, kernel, table, out):
    hre, him = coupled(tiles, kernel, table)
    field = inv_spectrum(hre, him, table)
    out[...] = field.astype(bf16).reshape(PEERS, ROWS, 128)


def sampled_body(first, tiles, kernel, table, spectrum, places, out, along_x, along_y):
    where = lax.broadcasted_iota(jnp.int32, (GRID, RECV), 0)
    at_x = jnp.where(where == places[0, 0:1, :], 1.0, 0.0).astype(bf16)
    at_y = jnp.where(where == places[0, 1:2, :], 1.0, 0.0).astype(bf16)
    start = pl.multiple_of(first[0], ROWS)
    xre = mm(table[0], at_x).astype(bf16)
    xim = mm(table[1], at_x).astype(bf16)
    yre = mm(table[0, pl.ds(start, ROWS), :], at_y)
    yim = mm(table[1, pl.ds(start, ROWS), :], at_y)
    along_x[0] = xre
    along_x[1] = xim
    along_y[0] = yre
    along_y[1] = yim
    hre, him = coupled(tiles, kernel, table)
    field = inv_spectrum(hre, him, table)
    out[:, 0:ROWS, :] = field.astype(bf16).reshape(PEERS, ROWS, 128)
    top = jnp.concatenate([hre[0:ROWS], him[0:ROWS]], axis=0).astype(bf16)
    top = jnp.concatenate([top, spectrum[0:ROWS], spectrum[64 : 64 + ROWS]], axis=0)
    a = mm(top, xre)
    b = mm(top, xim)
    a = a[0:64] + a[64:128]
    b = b[0:64] + b[64:128]
    pre = a[0:ROWS] - b[ROWS:64]
    pim = a[ROWS:64] + b[0:ROWS]
    sre = jnp.sum(pre * yre - pim * yim, axis=0, keepdims=True)
    sim = jnp.sum(pre * yim + pim * yre, axis=0, keepdims=True)
    total = jnp.concatenate([sre, sim], axis=1)
    high = total.astype(bf16).astype(f32)
    low = total - high
    row = lax.broadcasted_iota(jnp.int32, (16, 128), 0)
    extra = jnp.where(row == 0, high, jnp.where(row == 1, low, 0.0)).astype(bf16)
    for d in range(PEERS):
        out[d, ROWS : ROWS + 16, :] = extra


def back_body(tiles, kernel, table, measured, along_x, along_y, out):
    sums = jnp.zeros((16, 128), f32)
    for s in range(PEERS):
        sums = sums + tiles[s, ROWS : ROWS + 16, :].astype(f32)
    sums = sums[0:1] + sums[1:2]
    mre = sums[:, 0:RECV] - measured[0, 0:1, :]
    mim = sums[:, RECV : 2 * RECV] - measured[0, 1:2, :]
    yre = along_y[0]
    yim = along_y[1]
    mixed_re = mre * yre + mim * yim
    mixed_im = mim * yre - mre * yim
    mixed = jnp.concatenate([mixed_re, mixed_im], axis=0).astype(bf16)
    a = mm_nt(mixed, along_x[0])
    b = mm_nt(mixed, along_x[1])
    bre = (a[0:ROWS] + b[ROWS : 2 * ROWS]) * float(GRID)
    bim = (a[ROWS : 2 * ROWS] - b[0:ROWS]) * float(GRID)
    hre = []
    him = []
    for l in range(2):
        kre = kernel[0, 0, l].astype(f32)
        kim = kernel[1, 0, l].astype(f32)
        hre.append(kre * bre + kim * bim)
        him.append(kre * bim - kim * bre)
    field = inv_spectrum(jnp.concatenate(hre, axis=0), jnp.concatenate(him, axis=0), table)
    out[...] = field.astype(bf16).reshape(PEERS, ROWS, 128)


def field_body(tiles, incident, table, out):
    dre, dim = inv_lines(lines_of(tiles), table)
    for part, delta in enumerate((dre, dim)):
        total = incident[64 * part : 64 * part + 64] + delta
        for l in range(2):
            out[0, part, :, l, :] = total[ROWS * l : ROWS * l + ROWS]


def gradient_body(tiles, field_tiles, incident, table, wave, out):
    dre, dim = inv_lines(lines_of(field_tiles), table)
    ure = incident[0:64] + dre
    uim = incident[64:128] + dim
    wave[0:64] = ure
    wave[64:128] = uim
    bre, bim = inv_lines(lines_of(tiles), table)
    gre = (ure * bre + uim * bim).astype(bf16)
    gim = (ure * bim - uim * bre).astype(bf16)
    for s in range(PEERS):
        row = ROWS * (s // 4)
        part = gre if row < 64 else gim
        out[s] = part[row % 64 : row % 64 + ROWS, 128 * (s % 4) : 128 * (s % 4) + 128]


def share_body(arrived, out):
    total = jnp.zeros((ROWS, 128), f32)
    for s in range(PEERS):
        total = total + arrived[s].astype(f32)
    total = total.astype(bf16)
    for d in range(2 * PEERS):
        out[d] = total


def update_body(shares, contrast, wave, table, updated, out):
    freqs = 2.0 * PEERS
    rows = []
    for group in range(4):
        lanes = []
        for s in range(4 * group, 4 * group + 4):
            z = s // 2
            core = s % 2
            lanes.append(shares[4 * z + core].astype(f32) + shares[4 * z + 2 + core].astype(f32))
        total = jnp.concatenate(lanes, axis=1)
        new = contrast[ROWS * group : ROWS * group + ROWS] - total / freqs
        updated[group // 2, :, group % 2, :] = new
        rows.append(new)
    cre = jnp.concatenate(rows[0:2], axis=0)
    cim = jnp.concatenate(rows[2:4], axis=0)
    vre, vim = times(cre, cim, wave[0:64], wave[64:128])
    wre, wim = fwd_lines(vre, vim, table)
    store_tiles(out, wre, wim)


TILES = ((PEERS, ROWS, 128), bf16)
LINES = ((128, GRID), f32)
IN_VMEM = pl.BlockSpec(memory_space=pltpu.VMEM)
IN_SMEM = pl.BlockSpec(memory_space=pltpu.SMEM)


IN_HBM = pl.BlockSpec(memory_space=pltpu.HBM)


def run(body, outs, *args, spaces=(), scratch=()):
    many = isinstance(outs, list)
    shapes = [jax.ShapeDtypeStruct(*o) for o in (outs if many else [outs])]
    spaces = list(spaces) + [IN_VMEM] * (len(args) - len(spaces))
    return pl.pallas_call(
        body,
        out_shape=shapes if many else shapes[0],
        in_specs=spaces,
        out_specs=[IN_VMEM] * len(shapes) if many else IN_VMEM,
        scratch_shapes=scratch,
        compiler_params=pltpu.CompilerParams(vmem_limit_bytes=40 * 1024 * 1024),
    )(*args)


def exchange(blocks, axes):
    return lax.all_to_all(blocks, axes, split_axis=0, concat_axis=0, tiled=True)


def local(contrast, green_kernel, source_pos, receiver_pos, measured):
    table = jnp.asarray(dft_tables())
    kernel = green_kernel[0]
    first = (lax.axis_index("plane") * ROWS).astype(jnp.int32)[None]

    source, spectrum = run(
        source_body,
        [TILES, ((128, GRID), bf16)],
        source_pos,
        first,
        kernel,
        table,
        spaces=(IN_HBM, IN_SMEM, IN_HBM, IN_HBM),
        scratch=[
            pltpu.VMEM((2, 2, ROWS, GRID), bf16),
            pltpu.VMEM((2, GRID, GRID), bf16),
            pltpu.SMEM((1, 2), jnp.int32),
            pltpu.SemaphoreType.DMA((5,)),
        ],
    )
    arrived = exchange(source, "plane")
    incident, lines, sent = run(first_line_body, [LINES, LINES, TILES], arrived, contrast, table)
    arrived = exchange(sent, "plane")
    sent = run(spectral_body, TILES, arrived, kernel, table)
    arrived = exchange(sent, "plane")
    sent = run(line_body, TILES, arrived, lines, incident, table)
    arrived = exchange(sent, "plane")
    sent, along_x, along_y = run(
        sampled_body,
        [
            ((PEERS, ROWS + 16, 128), bf16),
            ((2, GRID, RECV), bf16),
            ((2, ROWS, RECV), f32),
        ],
        first,
        arrived,
        kernel,
        table,
        spectrum,
        receiver_pos,
        spaces=(IN_SMEM,),
    )
    field = exchange(sent, "plane")
    sent = run(back_body, TILES, field, kernel, table, measured, along_x, along_y)
    arrived = exchange(sent, "plane")
    wave, sent = run(gradient_body, [LINES, TILES], arrived, field, incident, table)
    arrived = exchange(sent, ("z", "core"))
    sent = run(share_body, ((2 * PEERS, ROWS, 128), bf16), arrived)
    arrived = exchange(sent, ("z", "yh", "core"))
    updated, sent = run(
        update_body, [(contrast.shape, f32), TILES], arrived, lines, wave, table
    )
    arrived = exchange(sent, "plane")
    sent = run(spectral_body, TILES, arrived, kernel, table)
    arrived = exchange(sent, "plane")
    field = run(field_body, ((1,) + contrast.shape, f32), arrived, incident, table)
    return updated, field


def solution(mesh):
    freqs = mesh.shape["freq"]
    split = Mesh(
        mesh.devices.reshape(freqs // 4, 2, 2, mesh.shape["plane"]), ("z", "yh", "core", "plane")
    )
    freq = ("z", "yh", "core")
    return jax.shard_map(
        local,
        mesh=split,
        in_specs=(
            P(None, "plane", None, None),
            P(freq, None, None, None, "plane", None),
            P(freq, None),
            P(freq, None, None),
            P(freq, None, None),
        ),
        out_specs=(P(None, "plane", None, None), P(freq, None, "plane", None, None)),
        check_vma=False,
    )
```

time: 160 us -> 153 us (0.956)
  blocking collectives: 74.2 us -> 138 us
  waiting for transfers between devices: 36.5 us -> 0 us
  starting transfers between devices: 28.5 us -> 0 us
  Pallas kernels: 13.8 us -> 9.77 us
    all_to_all x5 -> x10, blocking collectives: 74.2 us -> 138 us  [exchange(): return lax.all_to_all(blocks, axes, split_axis=0, concat_axis=0, tiled=True)]
    all_to_all x5 -> x0, waiting for transfers between devices: 36.5 us -> none  [exchange(): return lax.all_to_all(blocks, axes, split_axis=0, concat_axis=0, tiled=True)]
    all_to_all x5 -> x0, starting transfers between devices: 28.5 us -> none  [exchange(): return lax.all_to_all(blocks, axes, split_axis=0, concat_axis=0, tiled=True)]
    pallas_call x12 -> x11, Pallas kernels: 13.8 us -> 9.77 us  [run(): pl.pallas_call(body, out_shape=shapes if many else shapes[0], in_specs=sp...]
    reshape x3 -> x0, local copies, waits for them, and re-layouts: 1.89 us -> none  [the longest x2 1.81 us: by_row(): return lines.reshape(2, 2, ROWS, GRID).transpose(0, 2, 1, 3)]
  transfers between devices with their start and end apart: 5 -> 0, of which waited for: 5 -> 0; matrix products, arithmetic and copies ran while one was open for 1% -> 0% of each run, Pallas kernels for 0% -> 0%
where the time goes in v2:
time: 153 us
  blocking collectives  138 us (90%)
  Pallas kernels  9.77 us (6%)
  local copies, waits for them, and re-layouts  4.19 us (3%)
    all_to_all x10, blocking collectives, exchange(): return lax.all_to_all(blocks, axes, split_axis=0, concat_axis=0, tiled=True)  138 us
    pallas_call x11, Pallas kernels, run(): pl.pallas_call(body, out_shape=shapes if many else shapes[0], in_specs=sp...  9.77 us
    unnamed x16, local copies, waits for them, and re-layouts  4.19 us

profile of v2, /device:TPU:2, one launch (start us, length us, event | category | flops | bytes accessed | tf_op | source)
XLA Modules:
  0.0 152.6 jit_solution(5357023519691497559)
XLA Ops:
  1.3 1.2 copy-done
  2.5 0.9 copy-done.2
  3.5 1.3 shard_map.77
  4.8 16.1 %all_to_all.50.tiles = bf16[16,32,128]{2,1,0:T(8,128)(2,1)S(1)} all-to-all(bf16[16,32,128]{2,1,0:T(8,128)(2,1)S(1)} %get-tuple-element.14), channel_id=1, replica_groups=mesh['z'=8,'yh'=2,'core'=2,'plane'=16] {'plane'}, dimensions={0} | all-to-all | bytes 262144 | tf_op jit(solution)/shard_map/all_to_all | solution.py:340
  20.9 0.9 shard_map.78
  21.8 11.5 %all_to_all.51.tiles = bf16[16,32,128]{2,1,0:T(8,128)(2,1)S(1)} all-to-all(bf16[16,32,128]{2,1,0:T(8,128)(2,1)S(1)} %get-tuple-element.15), channel_id=1, replica_groups=mesh['z'=8,'yh'=2,'core'=2,'plane'=16] {'plane'}, dimensions={0} | all-to-all | bytes 262144 | tf_op jit(solution)/shard_map/all_to_all | solution.py:340
  33.3 0.9 shard_map.79
  34.1 11.5 %all_to_all.52.tiles = bf16[16,32,128]{2,1,0:T(8,128)(2,1)S(1)} all-to-all(bf16[16,32,128]{2,1,0:T(8,128)(2,1)S(1)} %shard_map.79), channel_id=1, replica_groups=mesh['z'=8,'yh'=2,'core'=2,'plane'=16] {'plane'}, dimensions={0} | all-to-all | bytes 262144 | tf_op jit(solution)/shard_map/all_to_all | solution.py:340
  45.7 0.9 shard_map.80
  46.6 11.5 %all_to_all.53.tiles = bf16[16,32,128]{2,1,0:T(8,128)(2,1)S(1)} all-to-all(bf16[16,32,128]{2,1,0:T(8,128)(2,1)S(1)} %shard_map.80), channel_id=1, replica_groups=mesh['z'=8,'yh'=2,'core'=2,'plane'=16] {'plane'}, dimensions={0} | all-to-all | bytes 262144 | tf_op jit(solution)/shard_map/all_to_all | solution.py:340
  58.1 0.7 copy-done.6
  58.8 1.4 shard_map.81
  60.2 12.1 %all_to_all.54.tiles.field_tiles = bf16[16,48,128]{2,1,0:T(8,128)(2,1)S(1)} all-to-all(bf16[16,48,128]{2,1,0:T(8,128)(2,1)S(1)} %get-tuple-element.19), channel_id=1, replica_groups=mesh['z'=8,'yh'=2,'core'=2,'plane'=16] {'plane'}, dimensions={0} | all-to-all | bytes 393216 | tf_op jit(solution)/shard_map/all_to_all | solution.py:340
  72.3 0.7 copy-done.5
  72.9 0.8 shard_map.82
  73.7 11.7 %all_to_all.55.tiles = bf16[16,32,128]{2,1,0:T(8,128)(2,1)S(1)} all-to-all(bf16[16,32,128]{2,1,0:T(8,128)(2,1)S(1)} %shard_map.82), channel_id=1, replica_groups=mesh['z'=8,'yh'=2,'core'=2,'plane'=16] {'plane'}, dimensions={0} | all-to-all | bytes 262144 | tf_op jit(solution)/shard_map/all_to_all | solution.py:340
  85.4 0.7 shard_map.83
  86.1 18.3 %all_to_all.56.arrived = bf16[16,32,128]{2,1,0:T(8,128)(2,1)S(1)} all-to-all(bf16[16,32,128]{2,1,0:T(8,128)(2,1)S(1)} %get-tuple-element.22), channel_id=1, replica_groups=mesh['z'=8,'yh'=2,'core'=2,'plane'=16] {'z','core'}, dimensions={0} | all-to-all | bytes 262144 | tf_op jit(solution)/shard_map/all_to_all | solution.py:340
  104.4 19.8 %all_to_all.57.shares = bf16[32,32,128]{2,1,0:T(8,128)(2,1)S(1)} all-to-all(bf16[32,32,128]{2,1,0:T(8,128)(2,1)S(1)} %shard_map.84), channel_id=1, replica_groups=mesh['z'=8,'yh'=2,'core'=2,'plane'=16] {'z','yh','core'}, dimensions={0} | all-to-all | bytes 524288 | tf_op jit(solution)/shard_map/all_to_all | solution.py:340
  124.2 0.9 shard_map.85
  125.1 13.7 %all_to_all.58.tiles = bf16[16,32,128]{2,1,0:T(8,128)(2,1)S(1)} all-to-all(bf16[16,32,128]{2,1,0:T(8,128)(2,1)S(1)} %get-tuple-element.25), channel_id=1, replica_groups=mesh['z'=8,'yh'=2,'core'=2,'plane'=16] {'plane'}, dimensions={0} | all-to-all | bytes 262144 | tf_op jit(solution)/shard_map/all_to_all | solution.py:340
  138.8 0.9 shard_map.86
  139.7 11.7 %all_to_all.59.tiles = bf16[16,32,128]{2,1,0:T(8,128)(2,1)S(1)} all-to-all(bf16[16,32,128]{2,1,0:T(8,128)(2,1)S(1)} %shard_map.86), channel_id=1, replica_groups=mesh['z'=8,'yh'=2,'core'=2,'plane'=16] {'plane'}, dimensions={0} | all-to-all | bytes 262144 | tf_op jit(solution)/shard_map/all_to_all | solution.py:340
  151.4 1.2 shard_map.87
  (13 shorter events, 0.7 us)
Async XLA Ops:
  0.6 0.7 copy-start.7
  1.3 1.2 copy-start
  2.5 0.9 copy-start.2
  3.5 17.4 %copy-start.1 = (bf16[2,512,512]{2,1,0:T(8,128)(2,1)S(1)}, bf16[2,512,512]{2,1,0:T(8,128)(2,1)}, u32[]{:S(2)}) copy-start(bf16[2,512,512]{2,1,0:T(8,128)(2,1)} %constant.8.clone.table_hbm.table) | copy-start | bytes 3145732
  4.7 16.1 %copy-start.4 = (f32[2,32,2,512]{3,2,1,0:T(2,128)S(1)}, f32[2,32,2,512]{3,2,1,0:T(2,128)}, u32[]{:S(2)}) copy-start(f32[2,32,2,512]{3,2,1,0:T(2,128)} %contrast.1) | copy-start | bytes 786436
  58.1 0.7 copy-start.6
  72.3 0.7 copy-start.5
  125.1 13.7 %copy-start.3 = (bf16[1,2,2,2,32,512]{5,4,3,2,1,0:T(8,128)(2,1)S(1)}, bf16[1,2,2,2,32,512]{5,4,3,2,1,0:T(8,128)(2,1)}, u32[]{:S(2)}) copy-start(bf16[1,2,2,2,32,512]{5,4,3,2,1,0:T(8,128)(2,1)} %param.7) | copy-start | bytes 786436

commit v3 on v2

--- a/solution.py
+++ b/solution.py
@@ -7,7 +7,6 @@
 from jax import lax
 from jax.experimental import pallas as pl
 from jax.experimental.pallas import tpu as pltpu
-from jax.sharding import Mesh
 from jax.sharding import PartitionSpec as P
 
 GRID = 512
@@ -17,6 +16,10 @@
 GAIN = 3.0
 f32 = jnp.float32
 bf16 = jnp.bfloat16
+
+ORDER = (4, 8, 5, 9, 7, 11, 6, 10, 0, 12, 1, 13, 3, 15, 2, 14)
+AT = tuple(ORDER.index(b) for b in range(PEERS))
+SHARES = tuple(2 * z + c for z in (0, 1, 7, 2, 6, 3, 5, 4) for c in (1, 0))
 
 
 def dft_tables():
@@ -53,7 +56,7 @@
 def lines_of(tiles):
     parts = [[], [], [], []]
     for g in range(4):
-        swapped = swap_groups([tiles[4 * g + i, 0:ROWS, :].astype(f32) for i in range(4)])
+        swapped = swap_groups([tiles[AT[4 * g + i], 0:ROWS, :].astype(f32) for i in range(4)])
         for j in range(4):
             parts[j].append(swapped[j])
     return jnp.concatenate([jnp.concatenate(p, axis=1) for p in parts], axis=0).astype(bf16)
@@ -64,7 +67,7 @@
     for g in range(4):
         swapped = swap_groups([q[:, 128 * g : 128 * g + 128] for q in quarter])
         for j in range(4):
-            out[4 * g + j] = swapped[j].astype(bf16)
+            out[AT[4 * g + j]] = swapped[j].astype(bf16)
 
 
 def inv_lines(lines, table):
@@ -88,6 +91,12 @@
     straight = jnp.concatenate([hre, him], axis=0).astype(bf16)
     crossed = jnp.concatenate([-him, hre], axis=0).astype(bf16)
     return mm_nt(table[0], straight) + mm_nt(table[1], crossed)
+
+
+def store_blocks(out, field):
+    field = field.astype(bf16)
+    for d in range(PEERS):
+        out[AT[d], 0:ROWS, :] = field[ROWS * d : ROWS * d + ROWS]
 
 
 def couple(kernel, fre, fim):
@@ -109,7 +118,22 @@
     return jnp.concatenate(hre, axis=0), jnp.concatenate(him, axis=0)
 
 
-def source_body(spot_hbm, first, kernel_hbm, table_hbm, out, spectrum, kernel, table, spot, sems):
+def source_body(
+    spot_hbm,
+    first,
+    kernel_hbm,
+    table_hbm,
+    places_hbm,
+    measured_hbm,
+    out,
+    spectrum,
+    table,
+    places,
+    measured,
+    kernel,
+    spot,
+    sems,
+):
     copies = []
     where = pltpu.make_async_copy(spot_hbm, spot, sems.at[4])
     where.start()
@@ -123,6 +147,12 @@
             pltpu.make_async_copy(table_hbm.at[part], table.at[part], sems.at[2 + part])
         )
     for copy in (copies[0], copies[2], copies[1], copies[3]):
+        copy.start()
+    extra = [
+        pltpu.make_async_copy(places_hbm, places, sems.at[5]),
+        pltpu.make_async_copy(measured_hbm, measured, sems.at[6]),
+    ]
+    for copy in extra:
         copy.start()
     where.wait()
     x0 = spot[0, 0]
@@ -155,7 +185,9 @@
     field = mm_nt(table[0], straight)
     copies[3].wait()
     field = field + mm_nt(table[1], crossed)
-    out[...] = field.astype(bf16).reshape(PEERS, ROWS, 128)
+    store_blocks(out, field)
+    for copy in extra:
+        copy.wait()
 
 
 def by_part_layer(field, part):
@@ -185,7 +217,8 @@
 
 
 def coupled(tiles, kernel, table):
-    turned = tiles[...].reshape(GRID, 128).astype(f32).T.astype(bf16)
+    stacked = jnp.concatenate([tiles[AT[d]] for d in range(PEERS)], axis=0)
+    turned = stacked.astype(f32).T.astype(bf16)
     a = mm(turned, table[0])
     b = mm(turned, table[1])
     fre = a[0:64] + b[64:128]
@@ -196,7 +229,7 @@
 def spectral_body(tiles, kernel, table, out):
     hre, him = coupled(tiles, kernel, table)
     field = inv_spectrum(hre, him, table)
-    out[...] = field.astype(bf16).reshape(PEERS, ROWS, 128)
+    store_blocks(out, field)
 
 
 def sampled_body(first, tiles, kernel, table, spectrum, places, out, along_x, along_y):
@@ -214,7 +247,7 @@
     along_y[1] = yim
     hre, him = coupled(tiles, kernel, table)
     field = inv_spectrum(hre, him, table)
-    out[:, 0:ROWS, :] = field.astype(bf16).reshape(PEERS, ROWS, 128)
+    store_blocks(out, field)
     top = jnp.concatenate([hre[0:ROWS], him[0:ROWS]], axis=0).astype(bf16)
     top = jnp.concatenate([top, spectrum[0:ROWS], spectrum[64 : 64 + ROWS]], axis=0)
     a = mm(top, xre)
@@ -258,7 +291,7 @@
         hre.append(kre * bre + kim * bim)
         him.append(kre * bim - kim * bre)
     field = inv_spectrum(jnp.concatenate(hre, axis=0), jnp.concatenate(him, axis=0), table)
-    out[...] = field.astype(bf16).reshape(PEERS, ROWS, 128)
+    store_blocks(out, field)
 
 
 def field_body(tiles, incident, table, out):
@@ -281,7 +314,7 @@
     for s in range(PEERS):
         row = ROWS * (s // 4)
         part = gre if row < 64 else gim
-        out[s] = part[row % 64 : row % 64 + ROWS, 128 * (s % 4) : 128 * (s % 4) + 128]
+        out[SHARES.index(s)] = part[row % 64 : row % 64 + ROWS, 128 * (s % 4) : 128 * (s % 4) + 128]
 
 
 def share_body(arrived, out):
@@ -336,8 +369,14 @@
     )(*args)
 
 
-def exchange(blocks, axes):
-    return lax.all_to_all(blocks, axes, split_axis=0, concat_axis=0, tiled=True)
+def stay(array):
+    return pltpu.with_memory_space_constraint(array, pltpu.HBM)
+
+
+def exchange(blocks, axis, groups):
+    return lax.all_to_all(
+        blocks, axis, split_axis=0, concat_axis=0, tiled=True, axis_index_groups=groups
+    )
 
 
 def local(contrast, green_kernel, source_pos, receiver_pos, measured):
@@ -345,28 +384,35 @@
     kernel = green_kernel[0]
     first = (lax.axis_index("plane") * ROWS).astype(jnp.int32)[None]
 
-    source, spectrum = run(
+    source, spectrum, table, places, observed = run(
         source_body,
-        [TILES, ((128, GRID), bf16)],
-        source_pos,
+        [
+            TILES,
+            ((128, GRID), bf16),
+            (table.shape, bf16),
+            (receiver_pos.shape, jnp.int32),
+            (measured.shape, f32),
+        ],
+        stay(source_pos),
         first,
-        kernel,
-        table,
-        spaces=(IN_HBM, IN_SMEM, IN_HBM, IN_HBM),
+        stay(kernel),
+        stay(table),
+        stay(receiver_pos),
+        stay(measured),
+        spaces=(IN_HBM, IN_SMEM, IN_HBM, IN_HBM, IN_HBM, IN_HBM),
         scratch=[
             pltpu.VMEM((2, 2, ROWS, GRID), bf16),
-            pltpu.VMEM((2, GRID, GRID), bf16),
             pltpu.SMEM((1, 2), jnp.int32),
-            pltpu.SemaphoreType.DMA((5,)),
+            pltpu.SemaphoreType.DMA((7,)),
         ],
     )
-    arrived = exchange(source, "plane")
+    arrived = exchange(source, "plane", [list(ORDER)])
     incident, lines, sent = run(first_line_body, [LINES, LINES, TILES], arrived, contrast, table)
-    arrived = exchange(sent, "plane")
+    arrived = exchange(sent, "plane", [list(ORDER)])
     sent = run(spectral_body, TILES, arrived, kernel, table)
-    arrived = exchange(sent, "plane")
+    arrived = exchange(sent, "plane", [list(ORDER)])
     sent = run(line_body, TILES, arrived, lines, incident, table)
-    arrived = exchange(sent, "plane")
+    arrived = exchange(sent, "plane", [list(ORDER)])
     sent, along_x, along_y = run(
         sampled_body,
         [
@@ -379,42 +425,37 @@
         kernel,
         table,
         spectrum,
-        receiver_pos,
+        places,
         spaces=(IN_SMEM,),
     )
-    field = exchange(sent, "plane")
-    sent = run(back_body, TILES, field, kernel, table, measured, along_x, along_y)
-    arrived = exchange(sent, "plane")
+    field = exchange(sent, "plane", [list(ORDER)])
+    sent = run(back_body, TILES, field, kernel, table, observed, along_x, along_y)
+    arrived = exchange(sent, "plane", [list(ORDER)])
     wave, sent = run(gradient_body, [LINES, TILES], arrived, field, incident, table)
-    arrived = exchange(sent, ("z", "core"))
+    arrived = exchange(sent, "freq", [[4 * (s // 2) + 2 * y + s % 2 for s in SHARES] for y in range(2)])
     sent = run(share_body, ((2 * PEERS, ROWS, 128), bf16), arrived)
-    arrived = exchange(sent, ("z", "yh", "core"))
+    arrived = exchange(sent, "freq", None)
     updated, sent = run(
         update_body, [(contrast.shape, f32), TILES], arrived, lines, wave, table
     )
-    arrived = exchange(sent, "plane")
+    arrived = exchange(sent, "plane", [list(ORDER)])
     sent = run(spectral_body, TILES, arrived, kernel, table)
-    arrived = exchange(sent, "plane")
+    arrived = exchange(sent, "plane", [list(ORDER)])
     field = run(field_body, ((1,) + contrast.shape, f32), arrived, incident, table)
     return updated, field
 
 
 def solution(mesh):
-    freqs = mesh.shape["freq"]
-    split = Mesh(
-        mesh.devices.reshape(freqs // 4, 2, 2, mesh.shape["plane"]), ("z", "yh", "core", "plane")
-    )
-    freq = ("z", "yh", "core")
     return jax.shard_map(
         local,
-        mesh=split,
+        mesh=mesh,
         in_specs=(
             P(None, "plane", None, None),
-            P(freq, None, None, None, "plane", None),
-            P(freq, None),
-            P(freq, None, None),
-            P(freq, None, None),
+            P("freq", None, None, None, "plane", None),
+            P("freq", None),
+            P("freq", None, None),
+            P("freq", None, None),
         ),
-        out_specs=(P(None, "plane", None, None), P(freq, None, "plane", None, None)),
+        out_specs=(P(None, "plane", None, None), P("freq", None, "plane", None, None)),
         check_vma=False,
     )

time: 153 us -> 143 us (0.935)
  blocking collectives: 138 us -> 131 us
  local copies, waits for them, and re-layouts: 4.19 us -> 0.01 us
    all_to_all x10, blocking collectives: 138 us -> 131 us  [exchange(): lax.all_to_all(blocks, axis, split_axis=0, concat_axis=0, tiled=True, axi...]
    unnamed x16 -> x4, local copies, waits for them, and re-layouts: 4.19 us -> 0.01 us
where the time goes in v3:
time: 143 us; the launch traced here: 142 us
  blocking collectives  131 us (92%)
  Pallas kernels  10.3 us (7%)
    all_to_all x10, blocking collectives, exchange(): lax.all_to_all(blocks, axis, split_axis=0, concat_axis=0, tiled=True, axi...  131 us
    pallas_call x11, Pallas kernels, run(): pl.pallas_call(body, out_shape=shapes if many else shapes[0], in_specs=sp...  10.3 us

profile of v3, /device:TPU:2, one launch (start us, length us, event | category | flops | bytes accessed | tf_op | source)
XLA Modules:
  0.0 142.1 jit_solution(17552929588977036534)
XLA Ops:
  0.6 1.8 %shard_map.77 = (bf16[16,32,128]{2,1,0:T(8,128)(2,1)S(1)}, bf16[128,512]{1,0:T(8,128)(2,1)S(1)}, bf16[2,512,512]{2,1,0:T(8,128)(2,1)S(1)}, s32[1,2,64]{2,1,0:T(2,128)S(1)}, f32[1,2,64]{2,1,0:T(2,128)S(1)}) custom-call(s32[1,2]{1,0:T(1,128)} %spot_hbm.1, s32[1]{0:T(128)} %bitcast.first, bf16[2,2,2,32,512]{4,3,2,1,0:T(8,128)(2,1)} %bitcast.2, ...), custom_call_target="tpu_custom_call" | custom-call | tf_op jit(solution)/shard_map/pallas_call | solution.py:362
  2.4 0.0 copy-start.1
  2.4 15.2 %all_to_all.50.tiles = bf16[16,32,128]{2,1,0:T(8,128)(2,1)S(1)} all-to-all(bf16[16,32,128]{2,1,0:T(8,128)(2,1)S(1)} %get-tuple-element.17), channel_id=1, replica_groups={{4,8,5,9,7,11,6,10,0,12,1,13,3,15,2,14},{20,24,21,25,23,27,22,26,16,28,..., dimensions={0} | all-to-all | bytes 262144 | tf_op jit(solution)/shard_map/all_to_all | solution.py:377
  17.6 0.0 copy-done.1
  17.6 0.9 shard_map.78
  18.5 0.0 copy-start
  18.5 10.9 %all_to_all.51.tiles = bf16[16,32,128]{2,1,0:T(8,128)(2,1)S(1)} all-to-all(bf16[16,32,128]{2,1,0:T(8,128)(2,1)S(1)} %get-tuple-element.19), channel_id=1, replica_groups={{4,8,5,9,7,11,6,10,0,12,1,13,3,15,2,14},{20,24,21,25,23,27,22,26,16,28,..., dimensions={0} | all-to-all | bytes 262144 | tf_op jit(solution)/shard_map/all_to_all | solution.py:377
  29.4 0.0 copy-done
  29.4 0.9 shard_map.79
  30.3 10.8 %all_to_all.52.tiles = bf16[16,32,128]{2,1,0:T(8,128)(2,1)S(1)} all-to-all(bf16[16,32,128]{2,1,0:T(8,128)(2,1)S(1)} %shard_map.79), channel_id=1, replica_groups={{4,8,5,9,7,11,6,10,0,12,1,13,3,15,2,14},{20,24,21,25,23,27,22,26,16,28,..., dimensions={0} | all-to-all | bytes 262144 | tf_op jit(solution)/shard_map/all_to_all | solution.py:377
  41.0 0.9 shard_map.80
  41.9 10.8 %all_to_all.53.tiles = bf16[16,32,128]{2,1,0:T(8,128)(2,1)S(1)} all-to-all(bf16[16,32,128]{2,1,0:T(8,128)(2,1)S(1)} %shard_map.80), channel_id=1, replica_groups={{4,8,5,9,7,11,6,10,0,12,1,13,3,15,2,14},{20,24,21,25,23,27,22,26,16,28,..., dimensions={0} | all-to-all | bytes 262144 | tf_op jit(solution)/shard_map/all_to_all | solution.py:377
  52.7 1.4 shard_map.81
  54.1 11.3 %all_to_all.54.tiles.field_tiles = bf16[16,48,128]{2,1,0:T(8,128)(2,1)S(1)} all-to-all(bf16[16,48,128]{2,1,0:T(8,128)(2,1)S(1)} %get-tuple-element.24), channel_id=1, replica_groups={{4,8,5,9,7,11,6,10,0,12,1,13,3,15,2,14},{20,24,21,25,23,27,22,26,16,28,..., dimensions={0} | all-to-all | bytes 393216 | tf_op jit(solution)/shard_map/all_to_all | solution.py:377
  65.4 0.8 shard_map.82
  66.2 10.8 %all_to_all.55.tiles = bf16[16,32,128]{2,1,0:T(8,128)(2,1)S(1)} all-to-all(bf16[16,32,128]{2,1,0:T(8,128)(2,1)S(1)} %shard_map.82), channel_id=1, replica_groups={{4,8,5,9,7,11,6,10,0,12,1,13,3,15,2,14},{20,24,21,25,23,27,22,26,16,28,..., dimensions={0} | all-to-all | bytes 262144 | tf_op jit(solution)/shard_map/all_to_all | solution.py:377
  77.0 0.7 shard_map.83
  77.7 18.9 %all_to_all.56.arrived = bf16[16,32,128]{2,1,0:T(8,128)(2,1)S(1)} all-to-all(bf16[16,32,128]{2,1,0:T(8,128)(2,1)S(1)} %get-tuple-element.28), channel_id=1, replica_groups={{16,0,80,64,464,448,144,128,400,384,208,192,336,320,272,256},{48,32,112..., dimensions={0} | all-to-all | bytes 262144 | tf_op jit(solution)/shard_map/all_to_all | solution.py:377
  96.6 19.2 %all_to_all.57.shares = bf16[32,32,128]{2,1,0:T(8,128)(2,1)S(1)} all-to-all(bf16[32,32,128]{2,1,0:T(8,128)(2,1)S(1)} %shard_map.84), channel_id=1, replica_groups=mesh['freq'=32,'plane'=16] {'freq'}, dimensions={0} | all-to-all | bytes 524288 | tf_op jit(solution)/shard_map/all_to_all | solution.py:377
  115.8 0.9 shard_map.85
  116.7 12.7 %all_to_all.58.tiles = bf16[16,32,128]{2,1,0:T(8,128)(2,1)S(1)} all-to-all(bf16[16,32,128]{2,1,0:T(8,128)(2,1)S(1)} %get-tuple-element.31), channel_id=1, replica_groups={{4,8,5,9,7,11,6,10,0,12,1,13,3,15,2,14},{20,24,21,25,23,27,22,26,16,28,..., dimensions={0} | all-to-all | bytes 262144 | tf_op jit(solution)/shard_map/all_to_all | solution.py:377
  129.3 0.9 shard_map.86
  130.2 10.7 %all_to_all.59.tiles = bf16[16,32,128]{2,1,0:T(8,128)(2,1)S(1)} all-to-all(bf16[16,32,128]{2,1,0:T(8,128)(2,1)S(1)} %shard_map.86), channel_id=1, replica_groups={{4,8,5,9,7,11,6,10,0,12,1,13,3,15,2,14},{20,24,21,25,23,27,22,26,16,28,..., dimensions={0} | all-to-all | bytes 262144 | tf_op jit(solution)/shard_map/all_to_all | solution.py:377
  140.9 1.2 shard_map.87
  (1 shorter events, 0.0 us)
Async XLA Ops:
  2.4 15.2 %copy-start.1 = (f32[2,32,2,512]{3,2,1,0:T(2,128)S(1)}, f32[2,32,2,512]{3,2,1,0:T(2,128)}, u32[]{:S(2)}) copy-start(f32[2,32,2,512]{3,2,1,0:T(2,128)} %contrast.1) | copy-start | bytes 786436
  18.5 10.9 %copy-start = (bf16[1,2,2,2,32,512]{5,4,3,2,1,0:T(8,128)(2,1)S(1)}, bf16[1,2,2,2,32,512]{5,4,3,2,1,0:T(8,128)(2,1)}, u32[]{:S(2)}) copy-start(bf16[1,2,2,2,32,512]{5,4,3,2,1,0:T(8,128)(2,1)} %param.7) | copy-start | bytes 786436

commit v4 on v3

--- a/solution.py
+++ b/solution.py
@@ -20,6 +20,8 @@
 ORDER = (4, 8, 5, 9, 7, 11, 6, 10, 0, 12, 1, 13, 3, 15, 2, 14)
 AT = tuple(ORDER.index(b) for b in range(PEERS))
 SHARES = tuple(2 * z + c for z in (0, 1, 7, 2, 6, 3, 5, 4) for c in (1, 0))
+
+FREQS = tuple(4 * z + 2 * y + c for z in (0, 4, 1, 5, 2, 6, 3, 7) for c in (1, 0) for y in (0, 1))
 
 
 def dft_tables():
@@ -218,7 +220,7 @@
 
 def coupled(tiles, kernel, table):
     stacked = jnp.concatenate([tiles[AT[d]] for d in range(PEERS)], axis=0)
-    turned = stacked.astype(f32).T.astype(bf16)
+    turned = stacked.T
     a = mm(turned, table[0])
     b = mm(turned, table[1])
     fre = a[0:64] + b[64:128]
@@ -261,16 +263,16 @@
     total = jnp.concatenate([sre, sim], axis=1)
     high = total.astype(bf16).astype(f32)
     low = total - high
-    row = lax.broadcasted_iota(jnp.int32, (16, 128), 0)
+    row = lax.broadcasted_iota(jnp.int32, (8, 128), 0)
     extra = jnp.where(row == 0, high, jnp.where(row == 1, low, 0.0)).astype(bf16)
     for d in range(PEERS):
-        out[d, ROWS : ROWS + 16, :] = extra
+        out[d, ROWS : ROWS + 8, :] = extra
 
 
 def back_body(tiles, kernel, table, measured, along_x, along_y, out):
-    sums = jnp.zeros((16, 128), f32)
+    sums = jnp.zeros((8, 128), f32)
     for s in range(PEERS):
-        sums = sums + tiles[s, ROWS : ROWS + 16, :].astype(f32)
+        sums = sums + tiles[s, ROWS : ROWS + 8, :].astype(f32)
     sums = sums[0:1] + sums[1:2]
     mre = sums[:, 0:RECV] - measured[0, 0:1, :]
     mim = sums[:, RECV : 2 * RECV] - measured[0, 1:2, :]
@@ -334,7 +336,8 @@
         for s in range(4 * group, 4 * group + 4):
             z = s // 2
             core = s % 2
-            lanes.append(shares[4 * z + core].astype(f32) + shares[4 * z + 2 + core].astype(f32))
+            pair = [shares[FREQS.index(4 * z + 2 * y + core)].astype(f32) for y in range(2)]
+            lanes.append(pair[0] + pair[1])
         total = jnp.concatenate(lanes, axis=1)
         new = contrast[ROWS * group : ROWS * group + ROWS] - total / freqs
         updated[group // 2, :, group % 2, :] = new
@@ -416,7 +419,7 @@
     sent, along_x, along_y = run(
         sampled_body,
         [
-            ((PEERS, ROWS + 16, 128), bf16),
+            ((PEERS, ROWS + 8, 128), bf16),
             ((2, GRID, RECV), bf16),
             ((2, ROWS, RECV), f32),
         ],
@@ -434,7 +437,7 @@
     wave, sent = run(gradient_body, [LINES, TILES], arrived, field, incident, table)
     arrived = exchange(sent, "freq", [[4 * (s // 2) + 2 * y + s % 2 for s in SHARES] for y in range(2)])
     sent = run(share_body, ((2 * PEERS, ROWS, 128), bf16), arrived)
-    arrived = exchange(sent, "freq", None)
+    arrived = exchange(sent, "freq", [list(FREQS)])
     updated, sent = run(
         update_body, [(contrast.shape, f32), TILES], arrived, lines, wave, table
     )

time: 143 us -> 142 us (level)
  the two profiles are of different devices: /device:TPU:2 before, /device:TPU:64 now
where the time goes in v4:
time: 142 us; the launch traced here: 141 us
  blocking collectives  130 us (92%)
  Pallas kernels  10.3 us (7%)
    all_to_all x10, blocking collectives, exchange(): lax.all_to_all(blocks, axis, split_axis=0, concat_axis=0, tiled=True, axi...  130 us
    pallas_call x11, Pallas kernels, run(): pl.pallas_call(body, out_shape=shapes if many else shapes[0], in_specs=sp...  10.3 us

profile of v4, /device:TPU:64, one launch (start us, length us, event | category | flops | bytes accessed | tf_op | source)
XLA Modules:
  0.0 141.1 jit_solution(3732474973557885231)
XLA Ops:
  0.6 1.8 %shard_map.77 = (bf16[16,32,128]{2,1,0:T(8,128)(2,1)S(1)}, bf16[128,512]{1,0:T(8,128)(2,1)S(1)}, bf16[2,512,512]{2,1,0:T(8,128)(2,1)S(1)}, s32[1,2,64]{2,1,0:T(2,128)S(1)}, f32[1,2,64]{2,1,0:T(2,128)S(1)}) custom-call(s32[1,2]{1,0:T(1,128)} %spot_hbm.1, s32[1]{0:T(128)} %bitcast.first, bf16[2,2,2,32,512]{4,3,2,1,0:T(8,128)(2,1)} %bitcast.2, ...), custom_call_target="tpu_custom_call" | custom-call | tf_op jit(solution)/shard_map/pallas_call | solution.py:365
  2.4 0.0 copy-start.1
  2.4 15.1 %all_to_all.50.tiles = bf16[16,32,128]{2,1,0:T(8,128)(2,1)S(1)} all-to-all(bf16[16,32,128]{2,1,0:T(8,128)(2,1)S(1)} %get-tuple-element.17), channel_id=1, replica_groups={{4,8,5,9,7,11,6,10,0,12,1,13,3,15,2,14},{20,24,21,25,23,27,22,26,16,28,..., dimensions={0} | all-to-all | bytes 262144 | tf_op jit(solution)/shard_map/all_to_all | solution.py:380
  17.5 0.0 copy-done.1
  17.5 0.9 shard_map.78
  18.4 0.0 copy-start
  18.4 10.9 %all_to_all.51.tiles = bf16[16,32,128]{2,1,0:T(8,128)(2,1)S(1)} all-to-all(bf16[16,32,128]{2,1,0:T(8,128)(2,1)S(1)} %get-tuple-element.19), channel_id=1, replica_groups={{4,8,5,9,7,11,6,10,0,12,1,13,3,15,2,14},{20,24,21,25,23,27,22,26,16,28,..., dimensions={0} | all-to-all | bytes 262144 | tf_op jit(solution)/shard_map/all_to_all | solution.py:380
  29.3 0.0 copy-done
  29.3 0.8 shard_map.79
  30.1 10.8 %all_to_all.52.tiles = bf16[16,32,128]{2,1,0:T(8,128)(2,1)S(1)} all-to-all(bf16[16,32,128]{2,1,0:T(8,128)(2,1)S(1)} %shard_map.79), channel_id=1, replica_groups={{4,8,5,9,7,11,6,10,0,12,1,13,3,15,2,14},{20,24,21,25,23,27,22,26,16,28,..., dimensions={0} | all-to-all | bytes 262144 | tf_op jit(solution)/shard_map/all_to_all | solution.py:380
  40.9 0.9 shard_map.80
  41.8 10.8 %all_to_all.53.tiles = bf16[16,32,128]{2,1,0:T(8,128)(2,1)S(1)} all-to-all(bf16[16,32,128]{2,1,0:T(8,128)(2,1)S(1)} %shard_map.80), channel_id=1, replica_groups={{4,8,5,9,7,11,6,10,0,12,1,13,3,15,2,14},{20,24,21,25,23,27,22,26,16,28,..., dimensions={0} | all-to-all | bytes 262144 | tf_op jit(solution)/shard_map/all_to_all | solution.py:380
  52.6 1.4 %shard_map.81 = (bf16[16,40,128]{2,1,0:T(8,128)(2,1)S(1)}, bf16[2,512,64]{2,1,0:T(8,128)(2,1)S(1)}, f32[2,32,64]{2,1,0:T(8,128)S(1)}) custom-call(s32[1]{0:T(128)} %bitcast.first, bf16[16,32,128]{2,1,0:T(8,128)(2,1)S(1)} %all_to_all.53.tiles, bf16[2,2,2,32,512]{4,3,2,1,0:T(8,128)(2,1)S(1)} %bitcast.4, bf16[2,512,512]{2,1,0:T(8,128)(2,1)S(1)} %get-tuple-element.18.table, ...), custom_call_target="tpu_custom_call" | custom-call | tf_op jit(solution)/shard_map/pallas_call | solution.py:365
  54.0 11.0 %all_to_all.54.tiles.field_tiles = bf16[16,40,128]{2,1,0:T(8,128)(2,1)S(1)} all-to-all(bf16[16,40,128]{2,1,0:T(8,128)(2,1)S(1)} %get-tuple-element.24), channel_id=1, replica_groups={{4,8,5,9,7,11,6,10,0,12,1,13,3,15,2,14},{20,24,21,25,23,27,22,26,16,28,..., dimensions={0} | all-to-all | bytes 327680 | tf_op jit(solution)/shard_map/all_to_all | solution.py:380
  65.0 0.8 shard_map.82
  65.7 10.7 %all_to_all.55.tiles = bf16[16,32,128]{2,1,0:T(8,128)(2,1)S(1)} all-to-all(bf16[16,32,128]{2,1,0:T(8,128)(2,1)S(1)} %shard_map.82), channel_id=1, replica_groups={{4,8,5,9,7,11,6,10,0,12,1,13,3,15,2,14},{20,24,21,25,23,27,22,26,16,28,..., dimensions={0} | all-to-all | bytes 262144 | tf_op jit(solution)/shard_map/all_to_all | solution.py:380
  76.5 0.7 shard_map.83
  77.2 17.0 %all_to_all.56.arrived = bf16[16,32,128]{2,1,0:T(8,128)(2,1)S(1)} all-to-all(bf16[16,32,128]{2,1,0:T(8,128)(2,1)S(1)} %get-tuple-element.28), channel_id=1, replica_groups={{16,0,80,64,464,448,144,128,400,384,208,192,336,320,272,256},{48,32,112..., dimensions={0} | all-to-all | bytes 262144 | tf_op jit(solution)/shard_map/all_to_all | solution.py:380
  94.2 20.3 %all_to_all.57.shares = bf16[32,32,128]{2,1,0:T(8,128)(2,1)S(1)} all-to-all(bf16[32,32,128]{2,1,0:T(8,128)(2,1)S(1)} %shard_map.84), channel_id=1, replica_groups={{16,48,0,32,272,304,256,288,80,112,64,96,336,368,320,352,144,176,128,16..., dimensions={0} | all-to-all | bytes 524288 | tf_op jit(solution)/shard_map/all_to_all | solution.py:380
  114.5 0.9 shard_map.85
  115.4 12.9 %all_to_all.58.tiles = bf16[16,32,128]{2,1,0:T(8,128)(2,1)S(1)} all-to-all(bf16[16,32,128]{2,1,0:T(8,128)(2,1)S(1)} %get-tuple-element.31), channel_id=1, replica_groups={{4,8,5,9,7,11,6,10,0,12,1,13,3,15,2,14},{20,24,21,25,23,27,22,26,16,28,..., dimensions={0} | all-to-all | bytes 262144 | tf_op jit(solution)/shard_map/all_to_all | solution.py:380
  128.3 0.8 shard_map.86
  129.1 10.8 %all_to_all.59.tiles = bf16[16,32,128]{2,1,0:T(8,128)(2,1)S(1)} all-to-all(bf16[16,32,128]{2,1,0:T(8,128)(2,1)S(1)} %shard_map.86), channel_id=1, replica_groups={{4,8,5,9,7,11,6,10,0,12,1,13,3,15,2,14},{20,24,21,25,23,27,22,26,16,28,..., dimensions={0} | all-to-all | bytes 262144 | tf_op jit(solution)/shard_map/all_to_all | solution.py:380
  139.9 1.2 shard_map.87
  (1 shorter events, 0.0 us)
Async XLA Ops:
  2.4 15.1 %copy-start.1 = (f32[2,32,2,512]{3,2,1,0:T(2,128)S(1)}, f32[2,32,2,512]{3,2,1,0:T(2,128)}, u32[]{:S(2)}) copy-start(f32[2,32,2,512]{3,2,1,0:T(2,128)} %contrast.1) | copy-start | bytes 786436
  18.4 10.9 %copy-start = (bf16[1,2,2,2,32,512]{5,4,3,2,1,0:T(8,128)(2,1)S(1)}, bf16[1,2,2,2,32,512]{5,4,3,2,1,0:T(8,128)(2,1)}, u32[]{:S(2)}) copy-start(bf16[1,2,2,2,32,512]{5,4,3,2,1,0:T(8,128)(2,1)} %param.7) | copy-start | bytes 786436

commit v5 on v4

--- a/solution.py
+++ b/solution.py
@@ -234,6 +234,13 @@
     store_blocks(out, field)
 
 
+def last_spectral_body(tiles, kernel, table, updated, out, updated_hbm, sem):
+    copy = pltpu.make_async_copy(updated, updated_hbm, sem)
+    copy.start()
+    spectral_body(tiles, kernel, table, out)
+    copy.wait()
+
+
 def sampled_body(first, tiles, kernel, table, spectrum, places, out, along_x, along_y):
     where = lax.broadcasted_iota(jnp.int32, (GRID, RECV), 0)
     at_x = jnp.where(where == places[0, 0:1, :], 1.0, 0.0).astype(bf16)
@@ -358,7 +365,7 @@
 IN_HBM = pl.BlockSpec(memory_space=pltpu.HBM)
 
 
-def run(body, outs, *args, spaces=(), scratch=()):
+def run(body, outs, *args, spaces=(), scratch=(), places=None):
     many = isinstance(outs, list)
     shapes = [jax.ShapeDtypeStruct(*o) for o in (outs if many else [outs])]
     spaces = list(spaces) + [IN_VMEM] * (len(args) - len(spaces))
@@ -366,7 +373,7 @@
         body,
         out_shape=shapes if many else shapes[0],
         in_specs=spaces,
-        out_specs=[IN_VMEM] * len(shapes) if many else IN_VMEM,
+        out_specs=places or ([IN_VMEM] * len(shapes) if many else IN_VMEM),
         scratch_shapes=scratch,
         compiler_params=pltpu.CompilerParams(vmem_limit_bytes=40 * 1024 * 1024),
     )(*args)
@@ -442,7 +449,16 @@
         update_body, [(contrast.shape, f32), TILES], arrived, lines, wave, table
     )
     arrived = exchange(sent, "plane", [list(ORDER)])
-    sent = run(spectral_body, TILES, arrived, kernel, table)
+    sent, updated = run(
+        last_spectral_body,
+        [TILES, (contrast.shape, f32)],
+        arrived,
+        kernel,
+        table,
+        updated,
+        scratch=[pltpu.SemaphoreType.DMA],
+        places=[IN_VMEM, IN_HBM],
+    )
     arrived = exchange(sent, "plane", [list(ORDER)])
     field = run(field_body, ((1,) + contrast.shape, f32), arrived, incident, table)
     return updated, field

time: 142 us -> 141 us (level)
  the two profiles are of different devices: /device:TPU:64 before, /device:TPU:2 now
where the time goes in v5:
time: 141 us
  blocking collectives  130 us (92%)
  Pallas kernels  9.94 us (7%)
    all_to_all x10, blocking collectives, exchange(): lax.all_to_all(blocks, axis, split_axis=0, concat_axis=0, tiled=True, axi...  130 us
    pallas_call x11, Pallas kernels, run(): pl.pallas_call(body, out_shape=shapes if many else shapes[0], in_specs=sp...  9.94 us

profile of v5, /device:TPU:2, one launch (start us, length us, event | category | flops | bytes accessed | tf_op | source)
XLA Modules:
  0.0 140.7 jit_solution(3994117853125306315)
XLA Ops:
  0.6 1.8 %shard_map.77 = (bf16[16,32,128]{2,1,0:T(8,128)(2,1)S(1)}, bf16[128,512]{1,0:T(8,128)(2,1)S(1)}, bf16[2,512,512]{2,1,0:T(8,128)(2,1)S(1)}, s32[1,2,64]{2,1,0:T(2,128)S(1)}, f32[1,2,64]{2,1,0:T(2,128)S(1)}) custom-call(s32[1,2]{1,0:T(1,128)} %spot_hbm.1, s32[1]{0:T(128)} %bitcast.first, bf16[2,2,2,32,512]{4,3,2,1,0:T(8,128)(2,1)} %bitcast.2, ...), custom_call_target="tpu_custom_call" | custom-call | tf_op jit(solution)/shard_map/pallas_call | solution.py:372
  2.4 0.0 copy-start.1
  2.4 15.2 %all_to_all.50.tiles = bf16[16,32,128]{2,1,0:T(8,128)(2,1)S(1)} all-to-all(bf16[16,32,128]{2,1,0:T(8,128)(2,1)S(1)} %get-tuple-element.19), channel_id=1, replica_groups={{4,8,5,9,7,11,6,10,0,12,1,13,3,15,2,14},{20,24,21,25,23,27,22,26,16,28,..., dimensions={0} | all-to-all | bytes 262144 | tf_op jit(solution)/shard_map/all_to_all | solution.py:387
  17.6 0.0 copy-done.1
  17.6 0.9 shard_map.78
  18.5 0.0 copy-start
  18.5 10.9 %all_to_all.51.tiles = bf16[16,32,128]{2,1,0:T(8,128)(2,1)S(1)} all-to-all(bf16[16,32,128]{2,1,0:T(8,128)(2,1)S(1)} %get-tuple-element.21), channel_id=1, replica_groups={{4,8,5,9,7,11,6,10,0,12,1,13,3,15,2,14},{20,24,21,25,23,27,22,26,16,28,..., dimensions={0} | all-to-all | bytes 262144 | tf_op jit(solution)/shard_map/all_to_all | solution.py:387
  29.4 0.0 copy-done
  29.4 0.8 shard_map.79
  30.3 10.8 %all_to_all.52.tiles = bf16[16,32,128]{2,1,0:T(8,128)(2,1)S(1)} all-to-all(bf16[16,32,128]{2,1,0:T(8,128)(2,1)S(1)} %shard_map.79), channel_id=1, replica_groups={{4,8,5,9,7,11,6,10,0,12,1,13,3,15,2,14},{20,24,21,25,23,27,22,26,16,28,..., dimensions={0} | all-to-all | bytes 262144 | tf_op jit(solution)/shard_map/all_to_all | solution.py:387
  41.0 0.9 shard_map.80
  41.9 10.8 %all_to_all.53.tiles = bf16[16,32,128]{2,1,0:T(8,128)(2,1)S(1)} all-to-all(bf16[16,32,128]{2,1,0:T(8,128)(2,1)S(1)} %shard_map.80), channel_id=1, replica_groups={{4,8,5,9,7,11,6,10,0,12,1,13,3,15,2,14},{20,24,21,25,23,27,22,26,16,28,..., dimensions={0} | all-to-all | bytes 262144 | tf_op jit(solution)/shard_map/all_to_all | solution.py:387
  52.7 1.4 %shard_map.81 = (bf16[16,40,128]{2,1,0:T(8,128)(2,1)S(1)}, bf16[2,512,64]{2,1,0:T(8,128)(2,1)S(1)}, f32[2,32,64]{2,1,0:T(8,128)S(1)}) custom-call(s32[1]{0:T(128)} %bitcast.first, bf16[16,32,128]{2,1,0:T(8,128)(2,1)S(1)} %all_to_all.53.tiles, bf16[2,2,2,32,512]{4,3,2,1,0:T(8,128)(2,1)S(1)} %bitcast.4, bf16[2,512,512]{2,1,0:T(8,128)(2,1)S(1)} %get-tuple-element.20.table, ...), custom_call_target="tpu_custom_call" | custom-call | tf_op jit(solution)/shard_map/pallas_call | solution.py:372
  54.1 11.0 %all_to_all.54.tiles.field_tiles = bf16[16,40,128]{2,1,0:T(8,128)(2,1)S(1)} all-to-all(bf16[16,40,128]{2,1,0:T(8,128)(2,1)S(1)} %get-tuple-element.26), channel_id=1, replica_groups={{4,8,5,9,7,11,6,10,0,12,1,13,3,15,2,14},{20,24,21,25,23,27,22,26,16,28,..., dimensions={0} | all-to-all | bytes 327680 | tf_op jit(solution)/shard_map/all_to_all | solution.py:387
  65.1 0.8 shard_map.82
  65.9 10.8 %all_to_all.55.tiles = bf16[16,32,128]{2,1,0:T(8,128)(2,1)S(1)} all-to-all(bf16[16,32,128]{2,1,0:T(8,128)(2,1)S(1)} %shard_map.82), channel_id=1, replica_groups={{4,8,5,9,7,11,6,10,0,12,1,13,3,15,2,14},{20,24,21,25,23,27,22,26,16,28,..., dimensions={0} | all-to-all | bytes 262144 | tf_op jit(solution)/shard_map/all_to_all | solution.py:387
  76.6 0.7 shard_map.83
  77.4 18.9 %all_to_all.56.arrived = bf16[16,32,128]{2,1,0:T(8,128)(2,1)S(1)} all-to-all(bf16[16,32,128]{2,1,0:T(8,128)(2,1)S(1)} %get-tuple-element.30), channel_id=1, replica_groups={{16,0,80,64,464,448,144,128,400,384,208,192,336,320,272,256},{48,32,112..., dimensions={0} | all-to-all | bytes 262144 | tf_op jit(solution)/shard_map/all_to_all | solution.py:387
  96.3 18.1 %all_to_all.57.shares = bf16[32,32,128]{2,1,0:T(8,128)(2,1)S(1)} all-to-all(bf16[32,32,128]{2,1,0:T(8,128)(2,1)S(1)} %shard_map.84), channel_id=1, replica_groups={{16,48,0,32,272,304,256,288,80,112,64,96,336,368,320,352,144,176,128,16..., dimensions={0} | all-to-all | bytes 524288 | tf_op jit(solution)/shard_map/all_to_all | solution.py:387
  114.4 0.5 shard_map.85
  115.0 12.9 %all_to_all.58.tiles = bf16[16,32,128]{2,1,0:T(8,128)(2,1)S(1)} all-to-all(bf16[16,32,128]{2,1,0:T(8,128)(2,1)S(1)} %get-tuple-element.32), channel_id=1, replica_groups={{4,8,5,9,7,11,6,10,0,12,1,13,3,15,2,14},{20,24,21,25,23,27,22,26,16,28,..., dimensions={0} | all-to-all | bytes 262144 | tf_op jit(solution)/shard_map/all_to_all | solution.py:387
  127.9 0.8 shard_map.86
  128.8 10.8 %all_to_all.59.tiles = bf16[16,32,128]{2,1,0:T(8,128)(2,1)S(1)} all-to-all(bf16[16,32,128]{2,1,0:T(8,128)(2,1)S(1)} %get-tuple-element.35), channel_id=1, replica_groups={{4,8,5,9,7,11,6,10,0,12,1,13,3,15,2,14},{20,24,21,25,23,27,22,26,16,28,..., dimensions={0} | all-to-all | bytes 262144 | tf_op jit(solution)/shard_map/all_to_all | solution.py:387
  139.5 1.2 shard_map.87
  (1 shorter events, 0.0 us)
Async XLA Ops:
  2.4 15.2 %copy-start.1 = (f32[2,32,2,512]{3,2,1,0:T(2,128)S(1)}, f32[2,32,2,512]{3,2,1,0:T(2,128)}, u32[]{:S(2)}) copy-start(f32[2,32,2,512]{3,2,1,0:T(2,128)} %contrast.1) | copy-start | bytes 786436
  18.5 10.9 %copy-start = (bf16[1,2,2,2,32,512]{5,4,3,2,1,0:T(8,128)(2,1)S(1)}, bf16[1,2,2,2,32,512]{5,4,3,2,1,0:T(8,128)(2,1)}, u32[]{:S(2)}) copy-start(bf16[1,2,2,2,32,512]{5,4,3,2,1,0:T(8,128)(2,1)} %param.7) | copy-start | bytes 786436

commit v6 on v5

--- a/solution.py
+++ b/solution.py
@@ -17,7 +17,7 @@
 f32 = jnp.float32
 bf16 = jnp.bfloat16
 
-ORDER = (4, 8, 5, 9, 7, 11, 6, 10, 0, 12, 1, 13, 3, 15, 2, 14)
+ORDER = (5, 12, 4, 3, 1, 13, 7, 0, 9, 2, 6, 11, 8, 15, 14, 10)
 AT = tuple(ORDER.index(b) for b in range(PEERS))
 SHARES = tuple(2 * z + c for z in (0, 1, 7, 2, 6, 3, 5, 4) for c in (1, 0))
 

time: 141 us -> 141 us (level)
  no operation moved by 1% of the time
where the time goes in v6:
time: 141 us; the launch traced here: 140 us
  blocking collectives  130 us (92%)
  Pallas kernels  9.94 us (7%)
    all_to_all x10, blocking collectives, exchange(): lax.all_to_all(blocks, axis, split_axis=0, concat_axis=0, tiled=True, axi...  130 us
    pallas_call x11, Pallas kernels, run(): pl.pallas_call(body, out_shape=shapes if many else shapes[0], in_specs=sp...  9.94 us

profile of v6, /device:TPU:2, one launch (start us, length us, event | category | flops | bytes accessed | tf_op | source)
XLA Modules:
  0.0 140.2 jit_solution(26107276957043166)
XLA Ops:
  0.6 1.8 %shard_map.77 = (bf16[16,32,128]{2,1,0:T(8,128)(2,1)S(1)}, bf16[128,512]{1,0:T(8,128)(2,1)S(1)}, bf16[2,512,512]{2,1,0:T(8,128)(2,1)S(1)}, s32[1,2,64]{2,1,0:T(2,128)S(1)}, f32[1,2,64]{2,1,0:T(2,128)S(1)}) custom-call(s32[1,2]{1,0:T(1,128)} %spot_hbm.1, s32[1]{0:T(128)} %bitcast.first, bf16[2,2,2,32,512]{4,3,2,1,0:T(8,128)(2,1)} %bitcast.2, ...), custom_call_target="tpu_custom_call" | custom-call | tf_op jit(solution)/shard_map/pallas_call | solution.py:372
  2.4 0.0 copy-start.1
  2.4 15.7 %all_to_all.50.tiles = bf16[16,32,128]{2,1,0:T(8,128)(2,1)S(1)} all-to-all(bf16[16,32,128]{2,1,0:T(8,128)(2,1)S(1)} %get-tuple-element.19), channel_id=1, replica_groups={{5,12,4,3,1,13,7,0,9,2,6,11,8,15,14,10},{21,28,20,19,17,29,23,16,25,18,..., dimensions={0} | all-to-all | bytes 262144 | tf_op jit(solution)/shard_map/all_to_all | solution.py:387
  18.1 0.0 copy-done.1
  18.1 0.9 shard_map.78
  19.1 0.0 copy-start
  19.1 10.8 %all_to_all.51.tiles = bf16[16,32,128]{2,1,0:T(8,128)(2,1)S(1)} all-to-all(bf16[16,32,128]{2,1,0:T(8,128)(2,1)S(1)} %get-tuple-element.21), channel_id=1, replica_groups={{5,12,4,3,1,13,7,0,9,2,6,11,8,15,14,10},{21,28,20,19,17,29,23,16,25,18,..., dimensions={0} | all-to-all | bytes 262144 | tf_op jit(solution)/shard_map/all_to_all | solution.py:387
  29.9 0.0 copy-done
  29.9 0.8 shard_map.79
  30.7 10.7 %all_to_all.52.tiles = bf16[16,32,128]{2,1,0:T(8,128)(2,1)S(1)} all-to-all(bf16[16,32,128]{2,1,0:T(8,128)(2,1)S(1)} %shard_map.79), channel_id=1, replica_groups={{5,12,4,3,1,13,7,0,9,2,6,11,8,15,14,10},{21,28,20,19,17,29,23,16,25,18,..., dimensions={0} | all-to-all | bytes 262144 | tf_op jit(solution)/shard_map/all_to_all | solution.py:387
  41.4 0.9 shard_map.80
  42.3 10.7 %all_to_all.53.tiles = bf16[16,32,128]{2,1,0:T(8,128)(2,1)S(1)} all-to-all(bf16[16,32,128]{2,1,0:T(8,128)(2,1)S(1)} %shard_map.80), channel_id=1, replica_groups={{5,12,4,3,1,13,7,0,9,2,6,11,8,15,14,10},{21,28,20,19,17,29,23,16,25,18,..., dimensions={0} | all-to-all | bytes 262144 | tf_op jit(solution)/shard_map/all_to_all | solution.py:387
  53.0 1.4 %shard_map.81 = (bf16[16,40,128]{2,1,0:T(8,128)(2,1)S(1)}, bf16[2,512,64]{2,1,0:T(8,128)(2,1)S(1)}, f32[2,32,64]{2,1,0:T(8,128)S(1)}) custom-call(s32[1]{0:T(128)} %bitcast.first, bf16[16,32,128]{2,1,0:T(8,128)(2,1)S(1)} %all_to_all.53.tiles, bf16[2,2,2,32,512]{4,3,2,1,0:T(8,128)(2,1)S(1)} %bitcast.4, bf16[2,512,512]{2,1,0:T(8,128)(2,1)S(1)} %get-tuple-element.20.table, ...), custom_call_target="tpu_custom_call" | custom-call | tf_op jit(solution)/shard_map/pallas_call | solution.py:372
  54.4 10.9 %all_to_all.54.tiles.field_tiles = bf16[16,40,128]{2,1,0:T(8,128)(2,1)S(1)} all-to-all(bf16[16,40,128]{2,1,0:T(8,128)(2,1)S(1)} %get-tuple-element.26), channel_id=1, replica_groups={{5,12,4,3,1,13,7,0,9,2,6,11,8,15,14,10},{21,28,20,19,17,29,23,16,25,18,..., dimensions={0} | all-to-all | bytes 327680 | tf_op jit(solution)/shard_map/all_to_all | solution.py:387
  65.3 0.8 shard_map.82
  66.1 10.8 %all_to_all.55.tiles = bf16[16,32,128]{2,1,0:T(8,128)(2,1)S(1)} all-to-all(bf16[16,32,128]{2,1,0:T(8,128)(2,1)S(1)} %shard_map.82), channel_id=1, replica_groups={{5,12,4,3,1,13,7,0,9,2,6,11,8,15,14,10},{21,28,20,19,17,29,23,16,25,18,..., dimensions={0} | all-to-all | bytes 262144 | tf_op jit(solution)/shard_map/all_to_all | solution.py:387
  76.9 0.7 shard_map.83
  77.6 18.0 %all_to_all.56.arrived = bf16[16,32,128]{2,1,0:T(8,128)(2,1)S(1)} all-to-all(bf16[16,32,128]{2,1,0:T(8,128)(2,1)S(1)} %get-tuple-element.30), channel_id=1, replica_groups={{16,0,80,64,464,448,144,128,400,384,208,192,336,320,272,256},{48,32,112..., dimensions={0} | all-to-all | bytes 262144 | tf_op jit(solution)/shard_map/all_to_all | solution.py:387
  95.6 18.1 %all_to_all.57.shares = bf16[32,32,128]{2,1,0:T(8,128)(2,1)S(1)} all-to-all(bf16[32,32,128]{2,1,0:T(8,128)(2,1)S(1)} %shard_map.84), channel_id=1, replica_groups={{16,48,0,32,272,304,256,288,80,112,64,96,336,368,320,352,144,176,128,16..., dimensions={0} | all-to-all | bytes 524288 | tf_op jit(solution)/shard_map/all_to_all | solution.py:387
  113.8 0.5 shard_map.85
  114.3 13.1 %all_to_all.58.tiles = bf16[16,32,128]{2,1,0:T(8,128)(2,1)S(1)} all-to-all(bf16[16,32,128]{2,1,0:T(8,128)(2,1)S(1)} %get-tuple-element.32), channel_id=1, replica_groups={{5,12,4,3,1,13,7,0,9,2,6,11,8,15,14,10},{21,28,20,19,17,29,23,16,25,18,..., dimensions={0} | all-to-all | bytes 262144 | tf_op jit(solution)/shard_map/all_to_all | solution.py:387
  127.5 0.8 shard_map.86
  128.3 10.7 %all_to_all.59.tiles = bf16[16,32,128]{2,1,0:T(8,128)(2,1)S(1)} all-to-all(bf16[16,32,128]{2,1,0:T(8,128)(2,1)S(1)} %get-tuple-element.35), channel_id=1, replica_groups={{5,12,4,3,1,13,7,0,9,2,6,11,8,15,14,10},{21,28,20,19,17,29,23,16,25,18,..., dimensions={0} | all-to-all | bytes 262144 | tf_op jit(solution)/shard_map/all_to_all | solution.py:387
  139.0 1.2 shard_map.87
  (1 shorter events, 0.0 us)
Async XLA Ops:
  2.4 15.7 %copy-start.1 = (f32[2,32,2,512]{3,2,1,0:T(2,128)S(1)}, f32[2,32,2,512]{3,2,1,0:T(2,128)}, u32[]{:S(2)}) copy-start(f32[2,32,2,512]{3,2,1,0:T(2,128)} %contrast.1) | copy-start | bytes 786436
  19.1 10.8 %copy-start = (bf16[1,2,2,2,32,512]{5,4,3,2,1,0:T(8,128)(2,1)S(1)}, bf16[1,2,2,2,32,512]{5,4,3,2,1,0:T(8,128)(2,1)}, u32[]{:S(2)}) copy-start(bf16[1,2,2,2,32,512]{5,4,3,2,1,0:T(8,128)(2,1)} %param.7) | copy-start | bytes 786436

commit v7 on v6

--- a/solution.py
+++ b/solution.py
@@ -19,9 +19,12 @@
 
 ORDER = (5, 12, 4, 3, 1, 13, 7, 0, 9, 2, 6, 11, 8, 15, 14, 10)
 AT = tuple(ORDER.index(b) for b in range(PEERS))
-SHARES = tuple(2 * z + c for z in (0, 1, 7, 2, 6, 3, 5, 4) for c in (1, 0))
-
-FREQS = tuple(4 * z + 2 * y + c for z in (0, 4, 1, 5, 2, 6, 3, 7) for c in (1, 0) for y in (0, 1))
+SHARES = tuple(2 * z + c for c in (1, 0) for z in range(8))
+
+FREQS = (
+    19, 28, 4, 5, 13, 29, 1, 17, 7, 25, 9, 8, 12, 14, 0, 24,
+    15, 2, 30, 23, 10, 20, 16, 22, 3, 27, 26, 11, 21, 18, 31, 6,
+)
 
 
 def dft_tables():

time: 141 us -> 138 us (0.979)
  the two profiles are of different devices: /device:TPU:2 before, /device:TPU:58 now
where the time goes in v7:
time: 138 us
  blocking collectives  127 us (92%)
  Pallas kernels  9.93 us (7%)
    all_to_all x10, blocking collectives, exchange(): lax.all_to_all(blocks, axis, split_axis=0, concat_axis=0, tiled=True, axi...  127 us
    pallas_call x11, Pallas kernels, run(): pl.pallas_call(body, out_shape=shapes if many else shapes[0], in_specs=sp...  9.93 us

profile of v7, /device:TPU:58, one launch (start us, length us, event | category | flops | bytes accessed | tf_op | source)
XLA Modules:
  0.0 137.8 jit_solution(15219220679739504267)
XLA Ops:
  0.6 1.8 %shard_map.77 = (bf16[16,32,128]{2,1,0:T(8,128)(2,1)S(1)}, bf16[128,512]{1,0:T(8,128)(2,1)S(1)}, bf16[2,512,512]{2,1,0:T(8,128)(2,1)S(1)}, s32[1,2,64]{2,1,0:T(2,128)S(1)}, f32[1,2,64]{2,1,0:T(2,128)S(1)}) custom-call(s32[1,2]{1,0:T(1,128)} %spot_hbm.1, s32[1]{0:T(128)} %bitcast.first, bf16[2,2,2,32,512]{4,3,2,1,0:T(8,128)(2,1)} %bitcast.2, ...), custom_call_target="tpu_custom_call" | custom-call | tf_op jit(solution)/shard_map/pallas_call | solution.py:375
  2.4 0.0 copy-start.1
  2.4 12.9 %all_to_all.50.tiles = bf16[16,32,128]{2,1,0:T(8,128)(2,1)S(1)} all-to-all(bf16[16,32,128]{2,1,0:T(8,128)(2,1)S(1)} %get-tuple-element.19), channel_id=1, replica_groups={{5,12,4,3,1,13,7,0,9,2,6,11,8,15,14,10},{21,28,20,19,17,29,23,16,25,18,..., dimensions={0} | all-to-all | bytes 262144 | tf_op jit(solution)/shard_map/all_to_all | solution.py:390
  15.4 0.0 copy-done.1
  15.4 0.9 shard_map.78
  16.3 0.0 copy-start
  16.3 10.8 %all_to_all.51.tiles = bf16[16,32,128]{2,1,0:T(8,128)(2,1)S(1)} all-to-all(bf16[16,32,128]{2,1,0:T(8,128)(2,1)S(1)} %get-tuple-element.21), channel_id=1, replica_groups={{5,12,4,3,1,13,7,0,9,2,6,11,8,15,14,10},{21,28,20,19,17,29,23,16,25,18,..., dimensions={0} | all-to-all | bytes 262144 | tf_op jit(solution)/shard_map/all_to_all | solution.py:390
  27.1 0.0 copy-done
  27.1 0.8 shard_map.79
  27.9 10.7 %all_to_all.52.tiles = bf16[16,32,128]{2,1,0:T(8,128)(2,1)S(1)} all-to-all(bf16[16,32,128]{2,1,0:T(8,128)(2,1)S(1)} %shard_map.79), channel_id=1, replica_groups={{5,12,4,3,1,13,7,0,9,2,6,11,8,15,14,10},{21,28,20,19,17,29,23,16,25,18,..., dimensions={0} | all-to-all | bytes 262144 | tf_op jit(solution)/shard_map/all_to_all | solution.py:390
  38.6 0.9 shard_map.80
  39.5 10.7 %all_to_all.53.tiles = bf16[16,32,128]{2,1,0:T(8,128)(2,1)S(1)} all-to-all(bf16[16,32,128]{2,1,0:T(8,128)(2,1)S(1)} %shard_map.80), channel_id=1, replica_groups={{5,12,4,3,1,13,7,0,9,2,6,11,8,15,14,10},{21,28,20,19,17,29,23,16,25,18,..., dimensions={0} | all-to-all | bytes 262144 | tf_op jit(solution)/shard_map/all_to_all | solution.py:390
  50.2 1.4 %shard_map.81 = (bf16[16,40,128]{2,1,0:T(8,128)(2,1)S(1)}, bf16[2,512,64]{2,1,0:T(8,128)(2,1)S(1)}, f32[2,32,64]{2,1,0:T(8,128)S(1)}) custom-call(s32[1]{0:T(128)} %bitcast.first, bf16[16,32,128]{2,1,0:T(8,128)(2,1)S(1)} %all_to_all.53.tiles, bf16[2,2,2,32,512]{4,3,2,1,0:T(8,128)(2,1)S(1)} %bitcast.4, bf16[2,512,512]{2,1,0:T(8,128)(2,1)S(1)} %get-tuple-element.20.table, ...), custom_call_target="tpu_custom_call" | custom-call | tf_op jit(solution)/shard_map/pallas_call | solution.py:375
  51.6 10.9 %all_to_all.54.tiles.field_tiles = bf16[16,40,128]{2,1,0:T(8,128)(2,1)S(1)} all-to-all(bf16[16,40,128]{2,1,0:T(8,128)(2,1)S(1)} %get-tuple-element.26), channel_id=1, replica_groups={{5,12,4,3,1,13,7,0,9,2,6,11,8,15,14,10},{21,28,20,19,17,29,23,16,25,18,..., dimensions={0} | all-to-all | bytes 327680 | tf_op jit(solution)/shard_map/all_to_all | solution.py:390
  62.5 0.8 shard_map.82
  63.3 10.7 %all_to_all.55.tiles = bf16[16,32,128]{2,1,0:T(8,128)(2,1)S(1)} all-to-all(bf16[16,32,128]{2,1,0:T(8,128)(2,1)S(1)} %shard_map.82), channel_id=1, replica_groups={{5,12,4,3,1,13,7,0,9,2,6,11,8,15,14,10},{21,28,20,19,17,29,23,16,25,18,..., dimensions={0} | all-to-all | bytes 262144 | tf_op jit(solution)/shard_map/all_to_all | solution.py:390
  74.0 0.7 shard_map.83
  74.7 18.4 %all_to_all.56.arrived = bf16[16,32,128]{2,1,0:T(8,128)(2,1)S(1)} all-to-all(bf16[16,32,128]{2,1,0:T(8,128)(2,1)S(1)} %get-tuple-element.30), channel_id=1, replica_groups={{16,80,144,208,272,336,400,464,0,64,128,192,256,320,384,448},{48,112,17..., dimensions={0} | all-to-all | bytes 262144 | tf_op jit(solution)/shard_map/all_to_all | solution.py:390
  93.1 18.5 %all_to_all.57.shares = bf16[32,32,128]{2,1,0:T(8,128)(2,1)S(1)} all-to-all(bf16[32,32,128]{2,1,0:T(8,128)(2,1)S(1)} %shard_map.84), channel_id=1, replica_groups={{304,448,64,80,208,464,16,272,112,400,144,128,192,224,0,384,240,32,480,..., dimensions={0} | all-to-all | bytes 524288 | tf_op jit(solution)/shard_map/all_to_all | solution.py:390
  111.6 0.5 shard_map.85
  112.2 12.8 %all_to_all.58.tiles = bf16[16,32,128]{2,1,0:T(8,128)(2,1)S(1)} all-to-all(bf16[16,32,128]{2,1,0:T(8,128)(2,1)S(1)} %get-tuple-element.32), channel_id=1, replica_groups={{5,12,4,3,1,13,7,0,9,2,6,11,8,15,14,10},{21,28,20,19,17,29,23,16,25,18,..., dimensions={0} | all-to-all | bytes 262144 | tf_op jit(solution)/shard_map/all_to_all | solution.py:390
  125.0 0.8 shard_map.86
  125.9 10.7 %all_to_all.59.tiles = bf16[16,32,128]{2,1,0:T(8,128)(2,1)S(1)} all-to-all(bf16[16,32,128]{2,1,0:T(8,128)(2,1)S(1)} %get-tuple-element.35), channel_id=1, replica_groups={{5,12,4,3,1,13,7,0,9,2,6,11,8,15,14,10},{21,28,20,19,17,29,23,16,25,18,..., dimensions={0} | all-to-all | bytes 262144 | tf_op jit(solution)/shard_map/all_to_all | solution.py:390
  136.6 1.2 shard_map.87
  (1 shorter events, 0.0 us)
Async XLA Ops:
  2.4 12.9 %copy-start.1 = (f32[2,32,2,512]{3,2,1,0:T(2,128)S(1)}, f32[2,32,2,512]{3,2,1,0:T(2,128)}, u32[]{:S(2)}) copy-start(f32[2,32,2,512]{3,2,1,0:T(2,128)} %contrast.1) | copy-start | bytes 786436
  16.3 10.8 %copy-start = (bf16[1,2,2,2,32,512]{5,4,3,2,1,0:T(8,128)(2,1)S(1)}, bf16[1,2,2,2,32,512]{5,4,3,2,1,0:T(8,128)(2,1)}, u32[]{:S(2)}) copy-start(bf16[1,2,2,2,32,512]{5,4,3,2,1,0:T(8,128)(2,1)} %param.7) | copy-start | bytes 786436

commit v8 on v7

--- a/solution.py
+++ b/solution.py
@@ -19,7 +19,7 @@
 
 ORDER = (5, 12, 4, 3, 1, 13, 7, 0, 9, 2, 6, 11, 8, 15, 14, 10)
 AT = tuple(ORDER.index(b) for b in range(PEERS))
-SHARES = tuple(2 * z + c for c in (1, 0) for z in range(8))
+SHARES = tuple(2 * z + c for c in (1, 0) for z in (7, 6, 5, 4, 3, 2, 1, 0))
 
 FREQS = (
     19, 28, 4, 5, 13, 29, 1, 17, 7, 25, 9, 8, 12, 14, 0, 24,

time: 138 us -> 137 us (level)
    all_to_all x10, blocking collectives: 127 us -> 126 us  [exchange(): lax.all_to_all(blocks, axis, split_axis=0, concat_axis=0, tiled=True, axi...]
where the time goes in v8:
time: 137 us; the launch traced here: 136 us
  blocking collectives  126 us (92%)
  Pallas kernels  9.94 us (7%)
    all_to_all x10, blocking collectives, exchange(): lax.all_to_all(blocks, axis, split_axis=0, concat_axis=0, tiled=True, axi...  126 us
    pallas_call x11, Pallas kernels, run(): pl.pallas_call(body, out_shape=shapes if many else shapes[0], in_specs=sp...  9.94 us

profile of v8, /device:TPU:58, one launch (start us, length us, event | category | flops | bytes accessed | tf_op | source)
XLA Modules:
  0.0 136.4 jit_solution(10640662526571284911)
XLA Ops:
  0.6 1.8 %shard_map.77 = (bf16[16,32,128]{2,1,0:T(8,128)(2,1)S(1)}, bf16[128,512]{1,0:T(8,128)(2,1)S(1)}, bf16[2,512,512]{2,1,0:T(8,128)(2,1)S(1)}, s32[1,2,64]{2,1,0:T(2,128)S(1)}, f32[1,2,64]{2,1,0:T(2,128)S(1)}) custom-call(s32[1,2]{1,0:T(1,128)} %spot_hbm.1, s32[1]{0:T(128)} %bitcast.first, bf16[2,2,2,32,512]{4,3,2,1,0:T(8,128)(2,1)} %bitcast.2, ...), custom_call_target="tpu_custom_call" | custom-call | tf_op jit(solution)/shard_map/pallas_call | solution.py:375
  2.4 0.0 copy-start.1
  2.4 12.9 %all_to_all.50.tiles = bf16[16,32,128]{2,1,0:T(8,128)(2,1)S(1)} all-to-all(bf16[16,32,128]{2,1,0:T(8,128)(2,1)S(1)} %get-tuple-element.19), channel_id=1, replica_groups={{5,12,4,3,1,13,7,0,9,2,6,11,8,15,14,10},{21,28,20,19,17,29,23,16,25,18,..., dimensions={0} | all-to-all | bytes 262144 | tf_op jit(solution)/shard_map/all_to_all | solution.py:390
  15.4 0.0 copy-done.1
  15.4 0.9 shard_map.78
  16.3 0.0 copy-start
  16.3 10.8 %all_to_all.51.tiles = bf16[16,32,128]{2,1,0:T(8,128)(2,1)S(1)} all-to-all(bf16[16,32,128]{2,1,0:T(8,128)(2,1)S(1)} %get-tuple-element.21), channel_id=1, replica_groups={{5,12,4,3,1,13,7,0,9,2,6,11,8,15,14,10},{21,28,20,19,17,29,23,16,25,18,..., dimensions={0} | all-to-all | bytes 262144 | tf_op jit(solution)/shard_map/all_to_all | solution.py:390
  27.1 0.0 copy-done
  27.1 0.8 shard_map.79
  27.9 10.7 %all_to_all.52.tiles = bf16[16,32,128]{2,1,0:T(8,128)(2,1)S(1)} all-to-all(bf16[16,32,128]{2,1,0:T(8,128)(2,1)S(1)} %shard_map.79), channel_id=1, replica_groups={{5,12,4,3,1,13,7,0,9,2,6,11,8,15,14,10},{21,28,20,19,17,29,23,16,25,18,..., dimensions={0} | all-to-all | bytes 262144 | tf_op jit(solution)/shard_map/all_to_all | solution.py:390
  38.6 0.9 shard_map.80
  39.5 10.7 %all_to_all.53.tiles = bf16[16,32,128]{2,1,0:T(8,128)(2,1)S(1)} all-to-all(bf16[16,32,128]{2,1,0:T(8,128)(2,1)S(1)} %shard_map.80), channel_id=1, replica_groups={{5,12,4,3,1,13,7,0,9,2,6,11,8,15,14,10},{21,28,20,19,17,29,23,16,25,18,..., dimensions={0} | all-to-all | bytes 262144 | tf_op jit(solution)/shard_map/all_to_all | solution.py:390
  50.2 1.4 %shard_map.81 = (bf16[16,40,128]{2,1,0:T(8,128)(2,1)S(1)}, bf16[2,512,64]{2,1,0:T(8,128)(2,1)S(1)}, f32[2,32,64]{2,1,0:T(8,128)S(1)}) custom-call(s32[1]{0:T(128)} %bitcast.first, bf16[16,32,128]{2,1,0:T(8,128)(2,1)S(1)} %all_to_all.53.tiles, bf16[2,2,2,32,512]{4,3,2,1,0:T(8,128)(2,1)S(1)} %bitcast.4, bf16[2,512,512]{2,1,0:T(8,128)(2,1)S(1)} %get-tuple-element.20.table, ...), custom_call_target="tpu_custom_call" | custom-call | tf_op jit(solution)/shard_map/pallas_call | solution.py:375
  51.6 10.9 %all_to_all.54.tiles.field_tiles = bf16[16,40,128]{2,1,0:T(8,128)(2,1)S(1)} all-to-all(bf16[16,40,128]{2,1,0:T(8,128)(2,1)S(1)} %get-tuple-element.26), channel_id=1, replica_groups={{5,12,4,3,1,13,7,0,9,2,6,11,8,15,14,10},{21,28,20,19,17,29,23,16,25,18,..., dimensions={0} | all-to-all | bytes 327680 | tf_op jit(solution)/shard_map/all_to_all | solution.py:390
  62.5 0.8 shard_map.82
  63.3 10.7 %all_to_all.55.tiles = bf16[16,32,128]{2,1,0:T(8,128)(2,1)S(1)} all-to-all(bf16[16,32,128]{2,1,0:T(8,128)(2,1)S(1)} %shard_map.82), channel_id=1, replica_groups={{5,12,4,3,1,13,7,0,9,2,6,11,8,15,14,10},{21,28,20,19,17,29,23,16,25,18,..., dimensions={0} | all-to-all | bytes 262144 | tf_op jit(solution)/shard_map/all_to_all | solution.py:390
  74.0 0.7 shard_map.83
  74.7 17.2 %all_to_all.56.arrived = bf16[16,32,128]{2,1,0:T(8,128)(2,1)S(1)} all-to-all(bf16[16,32,128]{2,1,0:T(8,128)(2,1)S(1)} %get-tuple-element.30), channel_id=1, replica_groups={{464,400,336,272,208,144,80,16,448,384,320,256,192,128,64,0},{496,432,3..., dimensions={0} | all-to-all | bytes 262144 | tf_op jit(solution)/shard_map/all_to_all | solution.py:390
  91.9 18.3 %all_to_all.57.shares = bf16[32,32,128]{2,1,0:T(8,128)(2,1)S(1)} all-to-all(bf16[32,32,128]{2,1,0:T(8,128)(2,1)S(1)} %shard_map.84), channel_id=1, replica_groups={{304,448,64,80,208,464,16,272,112,400,144,128,192,224,0,384,240,32,480,..., dimensions={0} | all-to-all | bytes 524288 | tf_op jit(solution)/shard_map/all_to_all | solution.py:390
  110.3 0.5 shard_map.85
  110.8 12.9 %all_to_all.58.tiles = bf16[16,32,128]{2,1,0:T(8,128)(2,1)S(1)} all-to-all(bf16[16,32,128]{2,1,0:T(8,128)(2,1)S(1)} %get-tuple-element.32), channel_id=1, replica_groups={{5,12,4,3,1,13,7,0,9,2,6,11,8,15,14,10},{21,28,20,19,17,29,23,16,25,18,..., dimensions={0} | all-to-all | bytes 262144 | tf_op jit(solution)/shard_map/all_to_all | solution.py:390
  123.7 0.8 shard_map.86
  124.5 10.7 %all_to_all.59.tiles = bf16[16,32,128]{2,1,0:T(8,128)(2,1)S(1)} all-to-all(bf16[16,32,128]{2,1,0:T(8,128)(2,1)S(1)} %get-tuple-element.35), channel_id=1, replica_groups={{5,12,4,3,1,13,7,0,9,2,6,11,8,15,14,10},{21,28,20,19,17,29,23,16,25,18,..., dimensions={0} | all-to-all | bytes 262144 | tf_op jit(solution)/shard_map/all_to_all | solution.py:390
  135.2 1.2 shard_map.87
  (1 shorter events, 0.0 us)
Async XLA Ops:
  2.4 12.9 %copy-start.1 = (f32[2,32,2,512]{3,2,1,0:T(2,128)S(1)}, f32[2,32,2,512]{3,2,1,0:T(2,128)}, u32[]{:S(2)}) copy-start(f32[2,32,2,512]{3,2,1,0:T(2,128)} %contrast.1) | copy-start | bytes 786436
  16.3 10.8 %copy-start = (bf16[1,2,2,2,32,512]{5,4,3,2,1,0:T(8,128)(2,1)S(1)}, bf16[1,2,2,2,32,512]{5,4,3,2,1,0:T(8,128)(2,1)}, u32[]{:S(2)}) copy-start(bf16[1,2,2,2,32,512]{5,4,3,2,1,0:T(8,128)(2,1)} %param.7) | copy-start | bytes 786436

commit v9 on v8

--- a/solution.py
+++ b/solution.py
@@ -19,7 +19,7 @@
 
 ORDER = (5, 12, 4, 3, 1, 13, 7, 0, 9, 2, 6, 11, 8, 15, 14, 10)
 AT = tuple(ORDER.index(b) for b in range(PEERS))
-SHARES = tuple(2 * z + c for c in (1, 0) for z in (7, 6, 5, 4, 3, 2, 1, 0))
+SHARES = tuple(2 * z + c for c in (0, 1) for z in (7, 6, 5, 4, 3, 2, 1, 0))
 
 FREQS = (
     19, 28, 4, 5, 13, 29, 1, 17, 7, 25, 9, 8, 12, 14, 0, 24,

time: 137 us -> 138 us (level)
  no operation moved by 1% of the time
where the time goes in v9:
time: 138 us
  blocking collectives  127 us (92%)
  Pallas kernels  9.93 us (7%)
    all_to_all x10, blocking collectives, exchange(): lax.all_to_all(blocks, axis, split_axis=0, concat_axis=0, tiled=True, axi...  127 us
    pallas_call x11, Pallas kernels, run(): pl.pallas_call(body, out_shape=shapes if many else shapes[0], in_specs=sp...  9.93 us

profile of v9, /device:TPU:58, one launch (start us, length us, event | category | flops | bytes accessed | tf_op | source)
XLA Modules:
  0.0 137.6 jit_solution(12431330884157047062)
XLA Ops:
  0.6 1.8 %shard_map.77 = (bf16[16,32,128]{2,1,0:T(8,128)(2,1)S(1)}, bf16[128,512]{1,0:T(8,128)(2,1)S(1)}, bf16[2,512,512]{2,1,0:T(8,128)(2,1)S(1)}, s32[1,2,64]{2,1,0:T(2,128)S(1)}, f32[1,2,64]{2,1,0:T(2,128)S(1)}) custom-call(s32[1,2]{1,0:T(1,128)} %spot_hbm.1, s32[1]{0:T(128)} %bitcast.first, bf16[2,2,2,32,512]{4,3,2,1,0:T(8,128)(2,1)} %bitcast.2, ...), custom_call_target="tpu_custom_call" | custom-call | tf_op jit(solution)/shard_map/pallas_call | solution.py:375
  2.4 0.0 copy-start.1
  2.4 12.9 %all_to_all.50.tiles = bf16[16,32,128]{2,1,0:T(8,128)(2,1)S(1)} all-to-all(bf16[16,32,128]{2,1,0:T(8,128)(2,1)S(1)} %get-tuple-element.19), channel_id=1, replica_groups={{5,12,4,3,1,13,7,0,9,2,6,11,8,15,14,10},{21,28,20,19,17,29,23,16,25,18,..., dimensions={0} | all-to-all | bytes 262144 | tf_op jit(solution)/shard_map/all_to_all | solution.py:390
  15.4 0.0 copy-done.1
  15.4 0.9 shard_map.78
  16.3 0.0 copy-start
  16.3 10.8 %all_to_all.51.tiles = bf16[16,32,128]{2,1,0:T(8,128)(2,1)S(1)} all-to-all(bf16[16,32,128]{2,1,0:T(8,128)(2,1)S(1)} %get-tuple-element.21), channel_id=1, replica_groups={{5,12,4,3,1,13,7,0,9,2,6,11,8,15,14,10},{21,28,20,19,17,29,23,16,25,18,..., dimensions={0} | all-to-all | bytes 262144 | tf_op jit(solution)/shard_map/all_to_all | solution.py:390
  27.1 0.0 copy-done
  27.1 0.8 shard_map.79
  27.9 10.7 %all_to_all.52.tiles = bf16[16,32,128]{2,1,0:T(8,128)(2,1)S(1)} all-to-all(bf16[16,32,128]{2,1,0:T(8,128)(2,1)S(1)} %shard_map.79), channel_id=1, replica_groups={{5,12,4,3,1,13,7,0,9,2,6,11,8,15,14,10},{21,28,20,19,17,29,23,16,25,18,..., dimensions={0} | all-to-all | bytes 262144 | tf_op jit(solution)/shard_map/all_to_all | solution.py:390
  38.6 0.9 shard_map.80
  39.5 10.7 %all_to_all.53.tiles = bf16[16,32,128]{2,1,0:T(8,128)(2,1)S(1)} all-to-all(bf16[16,32,128]{2,1,0:T(8,128)(2,1)S(1)} %shard_map.80), channel_id=1, replica_groups={{5,12,4,3,1,13,7,0,9,2,6,11,8,15,14,10},{21,28,20,19,17,29,23,16,25,18,..., dimensions={0} | all-to-all | bytes 262144 | tf_op jit(solution)/shard_map/all_to_all | solution.py:390
  50.2 1.4 %shard_map.81 = (bf16[16,40,128]{2,1,0:T(8,128)(2,1)S(1)}, bf16[2,512,64]{2,1,0:T(8,128)(2,1)S(1)}, f32[2,32,64]{2,1,0:T(8,128)S(1)}) custom-call(s32[1]{0:T(128)} %bitcast.first, bf16[16,32,128]{2,1,0:T(8,128)(2,1)S(1)} %all_to_all.53.tiles, bf16[2,2,2,32,512]{4,3,2,1,0:T(8,128)(2,1)S(1)} %bitcast.4, bf16[2,512,512]{2,1,0:T(8,128)(2,1)S(1)} %get-tuple-element.20.table, ...), custom_call_target="tpu_custom_call" | custom-call | tf_op jit(solution)/shard_map/pallas_call | solution.py:375
  51.6 10.9 %all_to_all.54.tiles.field_tiles = bf16[16,40,128]{2,1,0:T(8,128)(2,1)S(1)} all-to-all(bf16[16,40,128]{2,1,0:T(8,128)(2,1)S(1)} %get-tuple-element.26), channel_id=1, replica_groups={{5,12,4,3,1,13,7,0,9,2,6,11,8,15,14,10},{21,28,20,19,17,29,23,16,25,18,..., dimensions={0} | all-to-all | bytes 327680 | tf_op jit(solution)/shard_map/all_to_all | solution.py:390
  62.5 0.8 shard_map.82
  63.3 10.7 %all_to_all.55.tiles = bf16[16,32,128]{2,1,0:T(8,128)(2,1)S(1)} all-to-all(bf16[16,32,128]{2,1,0:T(8,128)(2,1)S(1)} %shard_map.82), channel_id=1, replica_groups={{5,12,4,3,1,13,7,0,9,2,6,11,8,15,14,10},{21,28,20,19,17,29,23,16,25,18,..., dimensions={0} | all-to-all | bytes 262144 | tf_op jit(solution)/shard_map/all_to_all | solution.py:390
  74.0 0.7 shard_map.83
  74.7 18.4 %all_to_all.56.arrived = bf16[16,32,128]{2,1,0:T(8,128)(2,1)S(1)} all-to-all(bf16[16,32,128]{2,1,0:T(8,128)(2,1)S(1)} %get-tuple-element.30), channel_id=1, replica_groups={{448,384,320,256,192,128,64,0,464,400,336,272,208,144,80,16},{480,416,3..., dimensions={0} | all-to-all | bytes 262144 | tf_op jit(solution)/shard_map/all_to_all | solution.py:390
  93.1 18.3 %all_to_all.57.shares = bf16[32,32,128]{2,1,0:T(8,128)(2,1)S(1)} all-to-all(bf16[32,32,128]{2,1,0:T(8,128)(2,1)S(1)} %shard_map.84), channel_id=1, replica_groups={{304,448,64,80,208,464,16,272,112,400,144,128,192,224,0,384,240,32,480,..., dimensions={0} | all-to-all | bytes 524288 | tf_op jit(solution)/shard_map/all_to_all | solution.py:390
  111.4 0.5 shard_map.85
  112.0 12.9 %all_to_all.58.tiles = bf16[16,32,128]{2,1,0:T(8,128)(2,1)S(1)} all-to-all(bf16[16,32,128]{2,1,0:T(8,128)(2,1)S(1)} %get-tuple-element.32), channel_id=1, replica_groups={{5,12,4,3,1,13,7,0,9,2,6,11,8,15,14,10},{21,28,20,19,17,29,23,16,25,18,..., dimensions={0} | all-to-all | bytes 262144 | tf_op jit(solution)/shard_map/all_to_all | solution.py:390
  124.8 0.8 shard_map.86
  125.7 10.7 %all_to_all.59.tiles = bf16[16,32,128]{2,1,0:T(8,128)(2,1)S(1)} all-to-all(bf16[16,32,128]{2,1,0:T(8,128)(2,1)S(1)} %get-tuple-element.35), channel_id=1, replica_groups={{5,12,4,3,1,13,7,0,9,2,6,11,8,15,14,10},{21,28,20,19,17,29,23,16,25,18,..., dimensions={0} | all-to-all | bytes 262144 | tf_op jit(solution)/shard_map/all_to_all | solution.py:390
  136.4 1.2 shard_map.87
  (1 shorter events, 0.0 us)
Async XLA Ops:
  2.4 12.9 %copy-start.1 = (f32[2,32,2,512]{3,2,1,0:T(2,128)S(1)}, f32[2,32,2,512]{3,2,1,0:T(2,128)}, u32[]{:S(2)}) copy-start(f32[2,32,2,512]{3,2,1,0:T(2,128)} %contrast.1) | copy-start | bytes 786436
  16.3 10.8 %copy-start = (bf16[1,2,2,2,32,512]{5,4,3,2,1,0:T(8,128)(2,1)S(1)}, bf16[1,2,2,2,32,512]{5,4,3,2,1,0:T(8,128)(2,1)}, u32[]{:S(2)}) copy-start(bf16[1,2,2,2,32,512]{5,4,3,2,1,0:T(8,128)(2,1)} %param.7) | copy-start | bytes 786436
